TPU v7x, 768 devices: a whole 4x8x12 slice. The times are simulated.
768 devices in a mesh: gx: 48 (over z, x), gy: 16 (over y, core).
Axes of the slice: x: 4, y: 8, z: 12, core: 2. Of those that a mesh axis runs over, the one named last changes fastest.
Arguments:
- electric: float32 [3, 1536, 256, 128], P(None, 'gx', 'gy'), may hold values from -6 to 6
- magnetic: float32 [3, 1536, 256, 128], P(None, 'gx', 'gy'), may hold values from -6 to 6
- material: int32 [1536, 256, 128], P('gx', 'gy'), may hold values from 0 to 3
- pml_flags: int32 [1536, 256, 128], P('gx', 'gy'), may hold values 0 or 1
- permittivity: float32 [4], replicated, may hold values from 1 to 12
- pml_sigma: float32 [128], replicated, may hold values from 0.05 to 1
- omega: float32 [8], replicated, may hold values from 0.5 to 3
Outputs:
- electric_out: float32 [3, 1536, 256, 128], P(None, 'gx', 'gy')
- magnetic_out: float32 [3, 1536, 256, 128], P(None, 'gx', 'gy')
- spectra: float32 [16, 2, 1536, 256], P('gy', None, 'gx')
All inputs are finite; a program needn't handle non-finite values. No bound on the sum of `pml_flags` on one device may be relied on, other than what follows from the above.
Results may differ from a plain program's by a relative error of at most 0.00002.
Values sent between devices are 32-bit elements; how exact they have to be, the bound alone decides.
No kernel may reach another device: no remote copies, remote signals or barrier semaphores. Data moves between devices by JAX's collectives and lax.ppermute only.
A program may use at most 32 MiB of HBM per device.

v0:
```python
import jax
import jax.numpy as jnp
from jax import lax
from jax.sharding import PartitionSpec as P

STEPS = 2
NFREQ = 8
NMAT = 4


time_step = 0.5


def from_behind(x, axis, by):
    devices = lax.axis_size(axis)
    pairs = [(i, i + by) for i in range(devices) if 0 <= i + by < devices]
    return lax.ppermute(x, axis, pairs)


def forward_diff(field, rim, axis):
    rest = lax.slice_in_dim(field, 1, field.shape[axis], axis=axis)
    return jnp.concatenate([rest, rim], axis=axis) - field


def backward_diff(field, rim, axis):
    rest = lax.slice_in_dim(field, 0, field.shape[axis] - 1, axis=axis)
    return field - jnp.concatenate([rim, rest], axis=axis)


def zero_rim(field, axis):
    return jnp.zeros_like(lax.slice_in_dim(field, 0, 1, axis=axis))


def coefficients(eps_cell, sigma_cell):
    s_mag = sigma_cell * time_step / 2.0
    h_keep = (1.0 - s_mag) / (1.0 + s_mag)
    h_gain = time_step / (1.0 + s_mag)
    s_ele = sigma_cell * time_step / (2.0 * eps_cell)
    e_keep = (1.0 - s_ele) / (1.0 + s_ele)
    e_gain = time_step / (eps_cell * (1.0 + s_ele))
    return (h_keep, h_gain, e_keep, e_gain)


def local(electric, magnetic, material, pml_flags, permittivity, pml_sigma, omega):
    eps_cell = jnp.zeros(material.shape, jnp.float32)
    for index in range(NMAT):
        eps_cell = eps_cell + (material == index).astype(jnp.float32) * permittivity[index]
    sigma_cell = pml_flags.astype(jnp.float32) * pml_sigma[None, None, :]
    plane_at = electric.shape[3] // 2
    slots_total = 2 * NFREQ
    coef_rows = []
    samples = []
    for step in range(STEPS):
        moment = (step + 1) * time_step
        coef_rows.append(jnp.concatenate([jnp.cos(omega * moment), -jnp.sin(omega * moment)]))
    h_keep, h_gain, e_keep, e_gain = coefficients(eps_cell, sigma_cell)
    for step in range(STEPS):
        ex, ey, ez = (electric[0], electric[1], electric[2])
        zero_z = zero_rim(ex, 2)
        rim_x = from_behind(jnp.stack([ey[:1], ez[:1]]), "gx", -1)
        rim_y = from_behind(jnp.stack([ex[:, :1], ez[:, :1]]), "gy", -1)
        curl_x = forward_diff(ez, rim_y[1], 1) - forward_diff(ey, zero_z, 2)
        curl_y = forward_diff(ex, zero_z, 2) - forward_diff(ez, rim_x[1], 0)
        curl_z = forward_diff(ey, rim_x[0], 0) - forward_diff(ex, rim_y[0], 1)
        magnetic = h_keep[None] * magnetic - h_gain[None] * jnp.stack([curl_x, curl_y, curl_z])
        hx, hy, hz = (magnetic[0], magnetic[1], magnetic[2])
        last_x = hx.shape[0] - 1
        last_y = hx.shape[1] - 1
        rim_hx = from_behind(jnp.stack([hy[last_x:], hz[last_x:]]), "gx", 1)
        rim_hy = from_behind(jnp.stack([hx[:, last_y:], hz[:, last_y:]]), "gy", 1)
        curl_x = backward_diff(hz, rim_hy[1], 1) - backward_diff(hy, zero_z, 2)
        curl_y = backward_diff(hx, zero_z, 2) - backward_diff(hz, rim_hx[1], 0)
        curl_z = backward_diff(hy, rim_hx[0], 0) - backward_diff(hx, rim_hy[0], 1)
        electric = e_keep[None] * electric + e_gain[None] * jnp.stack([curl_x, curl_y, curl_z])
        samples.append(electric[0:2, :, :, plane_at])
    coef_table = jnp.stack(coef_rows)
    partial_sums = jnp.zeros((slots_total,) + samples[0].shape, jnp.float32)
    for step in range(STEPS):
        partial_sums = partial_sums + coef_table[step][:, None, None, None] * samples[step][None]
    spectra = lax.all_to_all(partial_sums, "gy", split_axis=0, concat_axis=3, tiled=True)
    return (electric, magnetic, spectra)


def solution(mesh):
    placed = (
        P(None, "gx", "gy", None),
        P(None, "gx", "gy", None),
        P("gx", "gy", None),
        P("gx", "gy", None),
        P(),
        P(),
        P(),
    )
    return jax.shard_map(
        local,
        mesh=mesh,
        in_specs=placed,
        out_specs=(P(None, "gx", "gy", None), P(None, "gx", "gy", None), P("gy", None, "gx", None)),
        check_vma=False,
    )
```

profile of v0, /device:TPU:455, one launch (start us, length us, event | category | flops | bytes accessed | tf_op | source)
XLA Modules:
  0.0 76.1 jit_solution(37203810768451802)
XLA Ops:
  0.6 1.2 %fusion.27 = (f32[1,32,16,128]{3,2,1,0:T(8,128)S(1)}, f32[1,32,16,128]{3,2,1,0:T(8,128)S(1)}, f32[32,16,128]{2,1,0:T(8,128)S(1)}) fusion(f32[3,32,16,128]{3,2,1,0:T(8,128)} %param.7), kind=kLoop, calls=%fused_computation.91 | loop fusion | bytes 1572864 | tf_op jit(solution)/shard_map/slice | solution.py:58
  2.0 2.6 %collective-permute-start = (f32[2,32,1,128]{3,2,1,0:T(1,128)S(1)}, f32[2,32,1,128]{3,2,1,0:T(1,128)S(1)}, u32[]{:S(2)}, u32[]{:S(2)}) collective-permute-start(f32[2,32,1,128]{3,2,1,0:T(1,128)S(1)} %pad_maximum_fusion), channel_id=1, source_target_pairs={{1,0},{2,1},{3,2},{4,3},{5,4},{6,5},{7,6},{8,7},{9,8},{10,9},{11,1... | collective-permute-start | bytes 98312 | tf_op jit(solution)/shard_map/ppermute | solution.py:17
  4.7 2.5 %collective-permute-start.1 = (f32[2,1,16,128]{3,2,1,0:T(8,128)S(1)}, f32[2,1,16,128]{3,2,1,0:T(8,128)S(1)}, u32[]{:S(2)}, u32[]{:S(2)}) collective-permute-start(f32[2,1,16,128]{3,2,1,0:T(8,128)S(1)} %stack.100), channel_id=1, source_target_pairs={{16,0},{32,16},{48,32},{64,48},{80,64},{96,80},{112,96},{128,112},... | collective-permute-start | bytes 49160 | tf_op jit(solution)/shard_map/ppermute | solution.py:17
  9.2 2.8 %subtract_divide_fusion.1 = (f32[32,16,128]{2,1,0:T(8,128)S(1)}, f32[32,16,128]{2,1,0:T(8,128)S(1)}, f32[32,16,128]{2,1,0:T(8,128)S(1)}, f32[32,16,128]{2,1,0:T(8,128)S(1)}) fusion(f32[]{:T(128)} %bitcast.3, s32[32,16,128]{2,1,0:T(8,128)S(1)} %copy-done.22, f32[]{:T(128)} %bitcast.2, f32[]{:T(128)} %bitcast.1, f32[]{:T(128)} %bitcast, f32[128]{0:T(128)S(1)} %copy-done.25, ...), kind=kLoop, calls=%fused_computation.56 | loop fusion | flops 1703936 | bytes 1573392 | tf_op jit(solution)/shard_map/div | solution.py:39
  15.2 6.0 %collective-permute-start.3 = (f32[2,1,16,128]{3,2,1,0:T(8,128)S(1)}, f32[2,1,16,128]{3,2,1,0:T(8,128)S(1)}, u32[]{:S(2)}, u32[]{:S(2)}) collective-permute-start(f32[2,1,16,128]{3,2,1,0:T(8,128)S(1)} %stack.124), channel_id=1, source_target_pairs={{0,16},{16,32},{32,48},{48,64},{64,80},{80,96},{96,112},{112,128},... | collective-permute-start | bytes 49160 | tf_op jit(solution)/shard_map/ppermute | solution.py:17
  21.2 3.7 %collective-permute-start.2 = (f32[2,32,1,128]{3,1,2,0:T(8,128)S(1)}, f32[2,32,1,128]{3,1,2,0:T(8,128)S(1)}, u32[]{:S(2)}, u32[]{:S(2)}) collective-permute-start(f32[2,32,1,128]{3,1,2,0:T(8,128)S(1)} %pad_maximum_fusion.1), channel_id=1, source_target_pairs={{0,1},{1,2},{2,3},{3,4},{4,5},{5,6},{6,7},{7,8},{8,9},{9,10},{10,1... | collective-permute-start | bytes 98312 | tf_op jit(solution)/shard_map/ppermute | solution.py:17
  24.9 1.0 %collective-permute-done.2 = f32[2,32,1,128]{3,1,2,0:T(8,128)S(1)} collective-permute-done((f32[2,32,1,128]{3,1,2,0:T(8,128)S(1)}, f32[2,32,1,128]{3,1,2,0:T(8,128)S(1)}, u32[]{:S(2)}, u32[]{:S(2)}) %collective-permute-start.2) | collective-permute-done | bytes 32800 | tf_op jit(solution)/shard_map/ppermute | solution.py:17
  26.7 0.7 slice_bitcast_fusion.14
  27.4 0.8 %slice_bitcast_fusion.6 = (f32[31,16,128]{2,1,0:T(8,128)}, f32[1,31,16,128]{3,2,1,0:T(8,128)}) fusion(f32[3,32,16,128]{3,2,1,0:T(8,128)S(1)} %fusion.1), kind=kLoop, calls=%fused_computation.61 | loop fusion | bytes 1015808 | tf_op jit(solution)/shard_map/slice | solution.py:21
  28.2 0.8 %pad_subtract_fusion.1 = f32[32,16,128]{2,0,1:T(8,128)} fusion(f32[32,16,127]{2,0,1:T(8,128)S(1)} %slice.353, f32[1,32,16,128]{3,2,1,0:T(8,128)S(1)} %get-tuple-element.26), kind=kLoop, calls=%fused_computation.53 | loop fusion | flops 65536 | bytes 784384 | tf_op jit(solution)/shard_map/sub | solution.py:22
  29.1 1.9 %collective-permute-start.5 = (f32[2,1,16,128]{3,2,1,0:T(8,128)S(1)}, f32[2,1,16,128]{3,2,1,0:T(8,128)S(1)}, u32[]{:S(2)}, u32[]{:S(2)}) collective-permute-start(f32[2,1,16,128]{3,2,1,0:T(8,128)S(1)} %stack.125), channel_id=1, source_target_pairs={{16,0},{32,16},{48,32},{64,48},{80,64},{96,80},{112,96},{128,112},... | collective-permute-start | bytes 49160 | tf_op jit(solution)/shard_map/ppermute | solution.py:17
  31.0 0.7 slice.346
  31.7 1.0 %slice.375 = f32[2,32,16,1]{3,2,1,0:T(8,128)} slice(f32[3,32,16,128]{3,2,1,0:T(8,128)S(1)} %fusion.1), slice={[0:2], [0:32], [0:16], [64:65]} | slice | bytes 8192 | tf_op jit(solution)/shard_map/slice | solution.py:75
  32.7 1.9 %collective-permute-start.4 = (f32[2,32,1,128]{3,1,2,0:T(8,128)S(1)}, f32[2,32,1,128]{3,1,2,0:T(8,128)S(1)}, u32[]{:S(2)}, u32[]{:S(2)}) collective-permute-start(f32[2,32,1,128]{3,1,2,0:T(8,128)S(1)} %pad_maximum_fusion.2), channel_id=1, source_target_pairs={{1,0},{2,1},{3,2},{4,3},{5,4},{6,5},{7,6},{8,7},{9,8},{10,9},{11,1... | collective-permute-start | bytes 98312 | tf_op jit(solution)/shard_map/ppermute | solution.py:17
  34.7 1.3 %copy.119 = f32[2,32,16,1]{1,2,3,0:T(8,128)S(1)} copy(f32[2,32,16,1]{3,2,1,0:T(8,128)} %slice.375) | data formatting | bytes 8192 | tf_op jit(solution)/shard_map/slice | solution.py:75
  36.0 0.9 %collective-permute-done.5 = f32[2,1,16,128]{3,2,1,0:T(8,128)S(1)} collective-permute-done((f32[2,1,16,128]{3,2,1,0:T(8,128)S(1)}, f32[2,1,16,128]{3,2,1,0:T(8,128)S(1)}, u32[]{:S(2)}, u32[]{:S(2)}) %collective-permute-start.5) | collective-permute-done | bytes 16416 | tf_op jit(solution)/shard_map/ppermute | solution.py:17
  36.9 1.7 %collective-permute-done.4 = f32[2,32,1,128]{3,1,2,0:T(8,128)S(1)} collective-permute-done((f32[2,32,1,128]{3,1,2,0:T(8,128)S(1)}, f32[2,32,1,128]{3,1,2,0:T(8,128)S(1)}, u32[]{:S(2)}, u32[]{:S(2)}) %collective-permute-start.4) | collective-permute-done | bytes 32800 | tf_op jit(solution)/shard_map/ppermute | solution.py:17
  38.6 1.1 %maximum_subtract_fusion.11 = f32[1,32,16,128]{3,1,2,0:T(8,128)S(1)} fusion(f32[1,32,1,128]{3,1,2,0:T(8,128)S(1)} %get-tuple-element.52, f32[1,32,15,128]{3,1,2,0:T(8,128)} %slice_bitcast_fusion.14, f32[1,32,16,128]{3,2,1,0:T(8,128)S(1)} %get-tuple-element.26), kind=kLoop, calls=%fused_computation.39 | loop fusion | flops 131072 | bytes 786432 | tf_op jit(solution)/shard_map/sub | solution.py:22
  42.8 7.0 %collective-permute-start.7 = (f32[2,1,16,128]{3,2,1,0:T(8,128)S(1)}, f32[2,1,16,128]{3,2,1,0:T(8,128)S(1)}, u32[]{:S(2)}, u32[]{:S(2)}) collective-permute-start(f32[2,1,16,128]{3,2,1,0:T(8,128)S(1)} %stack.126), channel_id=1, source_target_pairs={{0,16},{16,32},{32,48},{48,64},{64,80},{80,96},{96,112},{112,128},... | collective-permute-start | bytes 49160 | tf_op jit(solution)/shard_map/ppermute | solution.py:17
  49.8 2.2 %collective-permute-start.6 = (f32[2,32,1,128]{3,1,2,0:T(8,128)S(1)}, f32[2,32,1,128]{3,1,2,0:T(8,128)S(1)}, u32[]{:S(2)}, u32[]{:S(2)}) collective-permute-start(f32[2,32,1,128]{3,1,2,0:T(8,128)S(1)} %pad_maximum_fusion.3), channel_id=1, source_target_pairs={{0,1},{1,2},{2,3},{3,4},{4,5},{5,6},{6,7},{7,8},{8,9},{9,10},{10,1... | collective-permute-start | bytes 98312 | tf_op jit(solution)/shard_map/ppermute | solution.py:17
  52.0 1.0 %collective-permute-done.6 = f32[2,32,1,128]{3,1,2,0:T(8,128)S(1)} collective-permute-done((f32[2,32,1,128]{3,1,2,0:T(8,128)S(1)}, f32[2,32,1,128]{3,1,2,0:T(8,128)S(1)}, u32[]{:S(2)}, u32[]{:S(2)}) %collective-permute-start.6) | collective-permute-done | bytes 32800 | tf_op jit(solution)/shard_map/ppermute | solution.py:17
  55.6 18.3 %all_to_all.18 = f32[16,1,1024]{2,1,0:T(1,128)S(1)} all-to-all(f32[16,1,1024]{2,1,0:T(1,128)S(1)} %reshape.67), channel_id=1, replica_groups=mesh['gx'=48,'gy'=16] {'gy'}, dimensions={0} | all-to-all | bytes 131072 | tf_op jit(solution)/shard_map/all_to_all | solution.py:80
  74.4 0.8 %reduce = f32[16,1024]{1,0:T(8,128)S(1)} reduce(f32[16,1,1024]{2,1,0:T(1,128)S(1)} %all_to_all.18, f32[]{:T(128)} %broadcast.76), dimensions={1}, to_apply=%all_to_all.13.reduce_sub_computation | reduce | bytes 131076 | tf_op jit(solution)/shard_map/all_to_all | solution.py:80
  75.4 0.7 copy.122
  (131 shorter events, 12.2 us)
Async XLA Ops:
  0.6 4.0 %copy-start = (f32[3,32,16,128]{3,2,1,0:T(8,128)S(1)}, f32[3,32,16,128]{3,2,1,0:T(8,128)}, u32[]{:S(2)}) copy-start(f32[3,32,16,128]{3,2,1,0:T(8,128)} %param.7) | copy-start | bytes 2359300
  2.0 10.8 %collective-permute-start = (f32[2,32,1,128]{3,2,1,0:T(1,128)S(1)}, f32[2,32,1,128]{3,2,1,0:T(1,128)S(1)}, u32[]{:S(2)}, u32[]{:S(2)}) collective-permute-start(f32[2,32,1,128]{3,2,1,0:T(1,128)S(1)} %pad_maximum_fusion), channel_id=1, source_target_pairs={{1,0},{2,1},{3,2},{4,3},{5,4},{6,5},{7,6},{8,7},{9,8},{10,9},{11,1... | collective-permute-start | bytes 98312 | tf_op jit(solution)/shard_map/ppermute | solution.py:17
  4.7 8.0 %collective-permute-start.1 = (f32[2,1,16,128]{3,2,1,0:T(8,128)S(1)}, f32[2,1,16,128]{3,2,1,0:T(8,128)S(1)}, u32[]{:S(2)}, u32[]{:S(2)}) collective-permute-start(f32[2,1,16,128]{3,2,1,0:T(8,128)S(1)} %stack.100), channel_id=1, source_target_pairs={{16,0},{32,16},{48,32},{64,48},{80,64},{96,80},{112,96},{128,112},... | collective-permute-start | bytes 49160 | tf_op jit(solution)/shard_map/ppermute | solution.py:17
  7.2 1.3 %copy-start.22 = (s32[32,16,128]{2,1,0:T(8,128)S(1)}, s32[32,16,128]{2,1,0:T(8,128)}, u32[]{:S(2)}) copy-start(s32[32,16,128]{2,1,0:T(8,128)} %param.9) | copy-start | bytes 786436
  7.2 1.3 %copy-start.23 = (s32[32,16,128]{2,1,0:T(8,128)S(1)}, s32[32,16,128]{2,1,0:T(8,128)}, u32[]{:S(2)}) copy-start(s32[32,16,128]{2,1,0:T(8,128)} %param.10) | copy-start | bytes 786436
  11.9 1.9 %copy-start.11 = (f32[32,16,128]{2,1,0:T(8,128)}, f32[32,16,128]{2,1,0:T(8,128)S(1)}, u32[]{:S(2)}) copy-start(f32[32,16,128]{2,1,0:T(8,128)S(1)} %get-tuple-element.43) | copy-start | bytes 786436
  11.9 1.9 %copy-start.13 = (f32[32,16,128]{2,1,0:T(8,128)}, f32[32,16,128]{2,1,0:T(8,128)S(1)}, u32[]{:S(2)}) copy-start(f32[32,16,128]{2,1,0:T(8,128)S(1)} %get-tuple-element.44) | copy-start | bytes 786436
  11.9 14.3 %copy-start.7 = (f32[32,16,128]{2,1,0:T(8,128)}, f32[32,16,128]{2,1,0:T(8,128)S(1)}, u32[]{:S(2)}) copy-start(f32[32,16,128]{2,1,0:T(8,128)S(1)} %get-tuple-element.41) | copy-start | bytes 786436
  11.9 14.3 %copy-start.9 = (f32[32,16,128]{2,1,0:T(8,128)}, f32[32,16,128]{2,1,0:T(8,128)S(1)}, u32[]{:S(2)}) copy-start(f32[32,16,128]{2,1,0:T(8,128)S(1)} %get-tuple-element.42) | copy-start | bytes 786436
  13.4 1.4 %copy-start.2 = (f32[3,32,16,128]{3,2,1,0:T(8,128)S(1)}, f32[3,32,16,128]{3,2,1,0:T(8,128)}, u32[]{:S(2)}) copy-start(f32[3,32,16,128]{3,2,1,0:T(8,128)} %param.8) | copy-start | bytes 2359300
  13.8 1.2 %copy-start.15 = (f32[1,32,16,128]{3,2,1,0:T(8,128)}, f32[1,32,16,128]{3,2,1,0:T(8,128)S(1)}, u32[]{:S(2)}) copy-start(f32[1,32,16,128]{3,2,1,0:T(8,128)S(1)} %fusion.8) | copy-start | bytes 786436
  15.2 9.7 %collective-permute-start.3 = (f32[2,1,16,128]{3,2,1,0:T(8,128)S(1)}, f32[2,1,16,128]{3,2,1,0:T(8,128)S(1)}, u32[]{:S(2)}, u32[]{:S(2)}) collective-permute-start(f32[2,1,16,128]{3,2,1,0:T(8,128)S(1)} %stack.124), channel_id=1, source_target_pairs={{0,16},{16,32},{32,48},{48,64},{64,80},{80,96},{96,112},{112,128},... | collective-permute-start | bytes 49160 | tf_op jit(solution)/shard_map/ppermute | solution.py:17
  21.2 4.7 %collective-permute-start.2 = (f32[2,32,1,128]{3,1,2,0:T(8,128)S(1)}, f32[2,32,1,128]{3,1,2,0:T(8,128)S(1)}, u32[]{:S(2)}, u32[]{:S(2)}) collective-permute-start(f32[2,32,1,128]{3,1,2,0:T(8,128)S(1)} %pad_maximum_fusion.1), channel_id=1, source_target_pairs={{0,1},{1,2},{2,3},{3,4},{4,5},{5,6},{6,7},{7,8},{8,9},{9,10},{10,1... | collective-permute-start | bytes 98312 | tf_op jit(solution)/shard_map/ppermute | solution.py:17
  29.1 7.8 %collective-permute-start.5 = (f32[2,1,16,128]{3,2,1,0:T(8,128)S(1)}, f32[2,1,16,128]{3,2,1,0:T(8,128)S(1)}, u32[]{:S(2)}, u32[]{:S(2)}) collective-permute-start(f32[2,1,16,128]{3,2,1,0:T(8,128)S(1)} %stack.125), channel_id=1, source_target_pairs={{16,0},{32,16},{48,32},{64,48},{80,64},{96,80},{112,96},{128,112},... | collective-permute-start | bytes 49160 | tf_op jit(solution)/shard_map/ppermute | solution.py:17
  32.7 5.8 %collective-permute-start.4 = (f32[2,32,1,128]{3,1,2,0:T(8,128)S(1)}, f32[2,32,1,128]{3,1,2,0:T(8,128)S(1)}, u32[]{:S(2)}, u32[]{:S(2)}) collective-permute-start(f32[2,32,1,128]{3,1,2,0:T(8,128)S(1)} %pad_maximum_fusion.2), channel_id=1, source_target_pairs={{1,0},{2,1},{3,2},{4,3},{5,4},{6,5},{7,6},{8,7},{9,8},{10,9},{11,1... | collective-permute-start | bytes 98312 | tf_op jit(solution)/shard_map/ppermute | solution.py:17
  38.5 1.1 %copy-start.20 = (f32[1,31,16,128]{3,2,1,0:T(8,128)S(1)}, f32[1,31,16,128]{3,2,1,0:T(8,128)}, u32[]{:S(2)}) copy-start(f32[1,31,16,128]{3,2,1,0:T(8,128)} %get-tuple-element.25) | copy-start | bytes 761860
  39.9 1.0 %copy-start.19 = (f32[32,15,128]{2,1,0:T(8,128)S(1)}, f32[32,15,128]{2,1,0:T(8,128)}, u32[]{:S(2)}) copy-start(f32[32,15,128]{2,1,0:T(8,128)} %slice.346) | copy-start | bytes 737284
  40.9 1.0 %copy-start.6 = (f32[1,32,16,128]{3,2,1,0:T(8,128)S(1)}, f32[1,32,16,128]{3,2,1,0:T(8,128)}, u32[]{:S(2)}) copy-start(f32[1,32,16,128]{3,2,1,0:T(8,128)} %copy-done.5) | copy-start | bytes 786436
  40.9 1.1 %copy-start.12 = (f32[32,16,128]{2,1,0:T(8,128)S(1)}, f32[32,16,128]{2,1,0:T(8,128)}, u32[]{:S(2)}) copy-start(f32[32,16,128]{2,1,0:T(8,128)} %copy-done.11) | copy-start | bytes 786436
  40.9 1.2 %copy-start.14 = (f32[32,16,128]{2,1,0:T(8,128)S(1)}, f32[32,16,128]{2,1,0:T(8,128)}, u32[]{:S(2)}) copy-start(f32[32,16,128]{2,1,0:T(8,128)} %copy-done.13) | copy-start | bytes 786436
  40.9 1.3 %copy-start.16 = (f32[1,32,16,128]{3,2,1,0:T(8,128)S(1)}, f32[1,32,16,128]{3,2,1,0:T(8,128)}, u32[]{:S(2)}) copy-start(f32[1,32,16,128]{3,2,1,0:T(8,128)} %copy-done.15) | copy-start | bytes 786436
  42.4 10.9 %copy-start.1 = (f32[3,32,16,128]{3,2,1,0:T(8,128)}, f32[3,32,16,128]{3,2,1,0:T(8,128)S(1)}, u32[]{:S(2)}) copy-start(f32[3,32,16,128]{3,2,1,0:T(8,128)S(1)} %fusion.2) | copy-start | bytes 2359300
  42.8 9.2 %collective-permute-start.7 = (f32[2,1,16,128]{3,2,1,0:T(8,128)S(1)}, f32[2,1,16,128]{3,2,1,0:T(8,128)S(1)}, u32[]{:S(2)}, u32[]{:S(2)}) collective-permute-start(f32[2,1,16,128]{3,2,1,0:T(8,128)S(1)} %stack.126), channel_id=1, source_target_pairs={{0,16},{16,32},{32,48},{48,64},{64,80},{80,96},{96,112},{112,128},... | collective-permute-start | bytes 49160 | tf_op jit(solution)/shard_map/ppermute | solution.py:17
  49.8 3.2 %collective-permute-start.6 = (f32[2,32,1,128]{3,1,2,0:T(8,128)S(1)}, f32[2,32,1,128]{3,1,2,0:T(8,128)S(1)}, u32[]{:S(2)}, u32[]{:S(2)}) collective-permute-start(f32[2,32,1,128]{3,1,2,0:T(8,128)S(1)} %pad_maximum_fusion.3), channel_id=1, source_target_pairs={{0,1},{1,2},{2,3},{3,4},{4,5},{5,6},{6,7},{7,8},{8,9},{9,10},{10,1... | collective-permute-start | bytes 98312 | tf_op jit(solution)/shard_map/ppermute | solution.py:17
  (11 other events, 9.1 us)
where the time goes:
time: 76.7 us; the launch traced here: 76.1 us
  starting transfers between devices  27.7 us (36%)
  blocking collectives  18.3 us (24%)
  local copies, waits for them, and re-layouts  15.5 us (20%)
  other arithmetic  8.53 us (11%)
  waiting for transfers between devices  4.68 us (6%)
  between operations  1.4 us (2%)
    ppermute x8, starting transfers between devices, from_behind(): return lax.ppermute(x, axis, pairs)  27.7 us
    all_to_all x1, blocking collectives, local(): lax.all_to_all(partial_sums, 'gy', split_axis=0, concat_axis=3, tiled=True)  18.3 us
    unnamed x64, local copies, waits for them, and re-layouts  6.88 us
    ppermute x8, waiting for transfers between devices, from_behind(): return lax.ppermute(x, axis, pairs)  4.68 us
    slice x4, local copies, waits for them, and re-layouts, local(): samples.append(electric[0:2, :, :, plane_at])  2.8 us
    div x1, other arithmetic, coefficients(): e_keep = (1.0 - s_ele) / (1.0 + s_ele)  2.75 us
    slice x8, local copies, waits for them, and re-layouts, forward_diff(): rest = lax.slice_in_dim(field, 1, field.shape[axis], axis=axis)  2.1 us
    sub x2, other arithmetic, forward_diff(): return jnp.concatenate([rest, rim], axis=axis) - field  1.92 us
  transfers between devices with their start and end apart: 8, of which 5 were waited for; matrix products, arithmetic and copies ran while one was open for 10% of the time, Pallas kernels for 0%

commit v1 on v0

v1 whole, which is shorter than its diff:
```python
import jax
import jax.numpy as jnp
from jax import lax
from jax.experimental import pallas as pl
from jax.experimental.pallas import tpu as pltpu
from jax.sharding import PartitionSpec as P

STEPS = 2
NFREQ = 8
NMAT = 4
time_step = 0.5

EX, EY, EZ, HX, HY, HZ, FL, MT = range(8)
ALL = tuple(range(8))
U_MSG = tuple((-1, f) for f in ALL) + tuple((-2, f) for f in (EX, EY, EZ, HX, HZ, FL))
D_MSG = tuple((0, f) for f in ALL) + tuple((1, f) for f in (EX, EZ))
R_MSG = tuple((-1, f) for f in ALL) + tuple((-2, f) for f in (EX, EY, EZ, HY, HZ, FL))
L_MSG = tuple((0, f) for f in ALL) + tuple((1, f) for f in (EY, EZ))


def shifted(x, axis, by):
    devices = lax.axis_size(axis)
    pairs = [(i, i + by) for i in range(devices) if 0 <= i + by < devices]
    return lax.ppermute(x, axis, pairs)


def field_plane(refs, f, x):
    e_ref, h_ref, m_ref, p_ref = refs
    if f < 3:
        return e_ref[f, x]
    if f < 6:
        return h_ref[f - 3, x]
    source = p_ref if f == FL else m_ref
    return source[x].astype(jnp.float32) + 1.0


def field_rows(refs, f, y):
    e_ref, h_ref, m_ref, p_ref = refs
    nx, ny = m_ref.shape[0], m_ref.shape[1]
    if f < 6:
        ref = e_ref if f < 3 else h_ref
        flat = ref.reshape(3 * nx * ny, 128)
        return flat[pl.ds((f % 3) * nx * ny + y, nx, stride=ny)]
    ref = p_ref if f == FL else m_ref
    return ref.reshape(nx * ny, 128)[pl.ds(y, nx, stride=ny)].astype(jnp.float32) + 1.0


def pack_rows_kernel(e_ref, h_ref, m_ref, p_ref, up_ref, down_ref):
    refs = (e_ref, h_ref, m_ref, p_ref)
    ny = m_ref.shape[1]
    for i, (at, f) in enumerate(U_MSG):
        up_ref[i] = field_rows(refs, f, ny + at)
    for i, (at, f) in enumerate(D_MSG):
        down_ref[i] = field_rows(refs, f, at)


def fill_third(third_ref, up_ref, down_ref, nx):
    flat = third_ref.reshape(8 * nx * 8, 128)
    for i, (at, f) in enumerate(U_MSG):
        flat[pl.ds(f * nx * 8 + 8 + at, nx, stride=8)] = up_ref[i]
    for i, (at, f) in enumerate(D_MSG):
        flat[pl.ds(f * nx * 8 + at, nx, stride=8)] = down_ref[i]


def pack_planes_kernel(e_ref, h_ref, m_ref, p_ref, up_ref, down_ref, right_ref, left_ref, third_ref):
    refs = (e_ref, h_ref, m_ref, p_ref)
    nx = m_ref.shape[0]
    fill_third(third_ref, up_ref, down_ref, nx)
    for message, ref, base in ((R_MSG, right_ref, nx), (L_MSG, left_ref, 0)):
        for i, (at, f) in enumerate(message):
            ref[i, 0:16] = field_plane(refs, f, base + at)
            ref[i, 16:24] = third_ref[f, base + at]


def next_y(a):
    return pltpu.roll(a, a.shape[0] - 1, 0)


def last_y(a):
    return pltpu.roll(a, 1, 0)


def window_kernel(e_ref, h_ref, m_ref, p_ref, up_ref, down_ref, right_ref, left_ref, sigma_ref, eps_ref, coef_ref,
                  eo_ref, ho_ref, part_ref, third_ref, first_ref, tile_ref):
    refs = (e_ref, h_ref, m_ref, p_ref)
    nx = m_ref.shape[0]
    fill_third(third_ref, up_ref, down_ref, nx)
    rows = (24, 128)
    lane = lax.broadcasted_iota(jnp.int32, rows, 1)
    not_last = lane != 127
    not_first = lane != 0
    sigma = sigma_ref[...]
    s_mag = sigma * time_step / 2.0
    h_keep_row = jnp.broadcast_to((1.0 - s_mag) / (1.0 + s_mag), rows)
    h_gain_row = jnp.broadcast_to(time_step / (1.0 + s_mag), rows)
    e_keep_rows, e_gain_rows, e_gain_free = [], [], []
    for k in range(NMAT):
        eps = jnp.full((1, 128), eps_ref[k], jnp.float32)
        s_ele = sigma * time_step / (2.0 * eps)
        e_keep_rows.append(jnp.broadcast_to((1.0 - s_ele) / (1.0 + s_ele), rows))
        e_gain_rows.append(jnp.broadcast_to(time_step / (eps * (1.0 + s_ele)), rows))
        e_gain_free.append(jnp.broadcast_to(time_step / eps, rows))

    def next_z(a):
        return jnp.where(not_last, pltpu.roll(a, 127, 1), 0.0)

    def last_z(a):
        return jnp.where(not_first, pltpu.roll(a, 1, 1), 0.0)

    def planes(x):
        if 0 <= x < nx:
            return [jnp.concatenate([field_plane(refs, f, x), third_ref[f, x]], axis=0) for f in ALL]
        message, ref, at = (R_MSG, right_ref, x) if x < 0 else (L_MSG, left_ref, x - nx)
        return [ref[message.index((at, f))] if (at, f) in message else None for f in ALL]

    def h_coefs(flag):
        keep = jnp.where(flag == 2.0, h_keep_row, 1.0)
        gain = jnp.where(flag == 2.0, h_gain_row, jnp.where(flag == 0.0, 0.0, time_step))
        return keep, gain

    def e_coefs(flag, code):
        m1, m2, m3 = code == 1.0, code == 2.0, code == 3.0

        def pick(table):
            return jnp.where(m1, table[0], jnp.where(m2, table[1], jnp.where(m3, table[2], table[3])))

        keep = jnp.where(flag == 2.0, pick(e_keep_rows), 1.0)
        gain = jnp.where(flag == 2.0, pick(e_gain_rows), pick(e_gain_free))
        return keep, jnp.where(code == 0.0, 0.0, gain)

    def h_step(h, e, e_next, coefs, with_x):
        keep, gain = coefs
        ex, ey, ez = e
        hx = None
        if with_x:
            hx = keep * h[0] - gain * ((next_y(ez) - ez) - (next_z(ey) - ey))
        hy = keep * h[1] - gain * ((next_z(ex) - ex) - (e_next[2] - ez))
        hz = keep * h[2] - gain * ((e_next[1] - ey) - (next_y(ex) - ex))
        return hx, hy, hz

    def e_step(e, h, h_last, coefs):
        keep, gain = coefs
        hx, hy, hz = h
        ex = keep * e[0] + gain * ((hz - last_y(hz)) - (hy - last_z(hy)))
        ey = keep * e[1] + gain * ((hx - last_z(hx)) - (hz - h_last[2]))
        ez = keep * e[2] + gain * ((hy - h_last[1]) - (hx - last_y(hx)))
        return ex, ey, ez

    here = planes(-2)
    h1_last = e1_last = h2_last = None
    hc_last = ec_last = None
    for x in range(-2, nx + 1):
        ahead = planes(x + 1)
        hc = h_coefs(here[FL])
        h1 = h_step(here[3:6], here[:3], ahead[:3], hc, x > -2)
        e1 = ec = None
        if x >= -1:
            ec = e_coefs(here[FL], here[MT])
            e1 = e_step(here[:3], h1, h1_last, ec)
            if 0 <= x < nx:
                first_ref[0, x] = e1[0][0:16]
                first_ref[1, x] = e1[1][0:16]
        if x >= 0:
            back = x - 1
            h2 = h_step(h1_last, e1_last, e1, hc_last, True)
            if back >= 0:
                e2 = e_step(e1_last, h2, h2_last, ec_last)
                for c in range(3):
                    ho_ref[c, back] = h2[c][0:16]
                    eo_ref[c, back] = e2[c][0:16]
            h2_last = h2
        here, h1_last, e1_last, hc_last, ec_last = ahead, h1, e1, hc, ec

    tile = (8, 128)
    lead = lax.broadcasted_iota(jnp.int32, tile, 1) - lax.broadcasted_iota(jnp.int32, tile, 0)
    for step, ref in enumerate((first_ref, eo_ref)):
        for low in range(8):
            total = jnp.zeros(tile, jnp.float32)
            for c in range(2):
                for high in range(nx // 8):
                    for half in range(2):
                        value = ref[c, high * 8 + low, half * 8:half * 8 + 8, :]
                        value = jnp.broadcast_to(value[:, 64:65], tile)
                        total = jnp.where(lead == (c * (nx // 8) + high) * 16 + half * 8, value, total)
            tile_ref[step, low:low + 1] = jnp.sum(total, axis=0, keepdims=True)
    for s in range(2 * NFREQ):
        part_ref[s] = coef_ref[0, s] * tile_ref[0] + coef_ref[1, s] * tile_ref[1]


def spectra_kernel(got_ref, out_ref):
    block = lax.broadcasted_iota(jnp.int32, (8, 128), 1) // 16
    for half in range(2):
        v = [got_ref[half * 8 + k] for k in range(8)]
        for bit in range(3):
            by = 1 << bit
            low_block = (block // by) % 2 == 0
            for a in range(8):
                if a & by:
                    continue
                low, high = v[a], v[a + by]
                v[a] = jnp.where(low_block, low, pltpu.roll(high, 16 * by, 1))
                v[a + by] = jnp.where(low_block, pltpu.roll(low, 128 - 16 * by, 1), high)
        for j in range(8):
            out_ref[0, j // 4, (j % 4) * 8:(j % 4) * 8 + 8, half * 128:half * 128 + 128] = v[j]


def shape(*dims):
    return jax.ShapeDtypeStruct(dims, jnp.float32)


VM = pl.BlockSpec(memory_space=pltpu.VMEM)
SM = pl.BlockSpec(memory_space=pltpu.SMEM)
LIMIT = pltpu.CompilerParams(vmem_limit_bytes=16 << 20)


def local(electric, magnetic, material, pml_flags, permittivity, pml_sigma, omega):
    nx, ny, nz = material.shape
    fields = (electric, magnetic, material, pml_flags)
    moments = jnp.arange(1, STEPS + 1, dtype=jnp.float32)[:, None] * time_step
    coef = jnp.concatenate([jnp.cos(omega[None] * moments), -jnp.sin(omega[None] * moments)], axis=1)

    up, down = pl.pallas_call(
        pack_rows_kernel,
        out_shape=(shape(len(U_MSG), nx, nz), shape(len(D_MSG), nx, nz)),
        in_specs=[VM] * 4, out_specs=(VM, VM), compiler_params=LIMIT,
    )(*fields)
    up, down = shifted(up, "gy", 1), shifted(down, "gy", -1)
    right, left = pl.pallas_call(
        pack_planes_kernel,
        out_shape=(shape(len(R_MSG), 24, nz), shape(len(L_MSG), 24, nz)),
        in_specs=[VM] * 6, out_specs=(VM, VM),
        scratch_shapes=[pltpu.VMEM((8, nx, 8, nz), jnp.float32)], compiler_params=LIMIT,
    )(*fields, up, down)
    right, left = shifted(right, "gx", 1), shifted(left, "gx", -1)
    electric_out, magnetic_out, part = pl.pallas_call(
        window_kernel,
        out_shape=(shape(3, nx, ny, nz), shape(3, nx, ny, nz), shape(2 * NFREQ, 8, 128)),
        in_specs=[VM] * 9 + [SM, SM], out_specs=(VM, VM, VM),
        scratch_shapes=[
            pltpu.VMEM((8, nx, 8, nz), jnp.float32),
            pltpu.VMEM((2, nx, ny, nz), jnp.float32),
            pltpu.VMEM((2, 8, 128), jnp.float32),
        ], compiler_params=LIMIT,
    )(*fields, up, down, right, left, pml_sigma[None], permittivity, coef)
    got = lax.all_to_all(part, "gy", split_axis=0, concat_axis=0, tiled=True)
    spectra = pl.pallas_call(
        spectra_kernel,
        out_shape=shape(1, 2, nx, 16 * ny),
        in_specs=[VM], out_specs=VM, compiler_params=LIMIT,
    )(got)
    return electric_out, magnetic_out, spectra


def solution(mesh):
    placed = (
        P(None, "gx", "gy", None),
        P(None, "gx", "gy", None),
        P("gx", "gy", None),
        P("gx", "gy", None),
        P(),
        P(),
        P(),
    )
    return jax.shard_map(
        local,
        mesh=mesh,
        in_specs=placed,
        out_specs=(P(None, "gx", "gy", None), P(None, "gx", "gy", None), P("gy", None, "gx", None)),
        check_vma=False,
    )
```

time: 76.7 us -> 54.2 us (0.71)
  the two profiles are of different devices: /device:TPU:455 before, /device:TPU:513 now
where the time goes in v1:
time: 54.2 us; the launch traced here: 53.9 us
  blocking collectives  16.3 us (30%)
  starting transfers between devices  13.2 us (24%)
  waiting for transfers between devices  12 us (22%)
  Pallas kernels  7.21 us (13%)
  local copies, waits for them, and re-layouts  4.17 us (8%)
  between operations  0.71 us (1%)
    all_to_all x1, blocking collectives, local(): got = lax.all_to_all(part, 'gy', split_axis=0, concat_axis=0, tiled=True)  16.3 us
    ppermute x4, starting transfers between devices, shifted(): return lax.ppermute(x, axis, pairs)  13.2 us
    ppermute x4, waiting for transfers between devices, shifted(): return lax.ppermute(x, axis, pairs)  12 us
    pallas_call x1, Pallas kernels, local(): pl.pallas_call(window_kernel, out_shape=(shape(3, nx, ny, nz), shape(3, n...  6.13 us
    unnamed x14, local copies, waits for them, and re-layouts  4.17 us
  transfers between devices with their start and end apart: 4, of which 2 were waited for; matrix products, arithmetic and copies ran while one was open for 0% of the time, Pallas kernels for 0%

profile of v1, /device:TPU:513, one launch (start us, length us, event | category | flops | bytes accessed | tf_op | source)
XLA Modules:
  0.0 53.9 jit_solution(16678009947650020076)
XLA Ops:
  0.6 0.0 copy-start
  0.6 1.1 %copy-done = f32[3,32,16,128]{3,2,1,0:T(8,128)S(1)} copy-done((f32[3,32,16,128]{3,2,1,0:T(8,128)S(1)}, f32[3,32,16,128]{3,2,1,0:T(8,128)}, u32[]{:S(2)}) %copy-start) | copy-done | bytes 786456
  1.8 0.0 copy-start.1
  1.8 1.1 %copy-done.1 = f32[3,32,16,128]{3,2,1,0:T(8,128)S(1)} copy-done((f32[3,32,16,128]{3,2,1,0:T(8,128)S(1)}, f32[3,32,16,128]{3,2,1,0:T(8,128)}, u32[]{:S(2)}) %copy-start.1) | copy-done | bytes 786456
  2.9 0.9 %copy-done.2 = s32[32,16,128]{2,1,0:T(8,128)S(1)} copy-done((s32[32,16,128]{2,1,0:T(8,128)S(1)}, s32[32,16,128]{2,1,0:T(8,128)}, u32[]{:S(2)}) %copy-start.2) | copy-done | bytes 262168
  3.9 0.9 %copy-done.3 = s32[32,16,128]{2,1,0:T(8,128)S(1)} copy-done((s32[32,16,128]{2,1,0:T(8,128)S(1)}, s32[32,16,128]{2,1,0:T(8,128)}, u32[]{:S(2)}) %copy-start.3) | copy-done | bytes 262168
  4.8 0.2 shard_map.94
  5.0 3.8 %collective-permute-start = (f32[14,32,128]{2,1,0:T(8,128)S(1)}, f32[14,32,128]{2,1,0:T(8,128)S(1)}, u32[]{:S(2)}, u32[]{:S(2)}) collective-permute-start(f32[14,32,128]{2,1,0:T(8,128)S(1)} %get-tuple-element.10), channel_id=1, source_target_pairs={{0,1},{1,2},{2,3},{3,4},{4,5},{5,6},{6,7},{7,8},{8,9},{9,10},{10,1... | collective-permute-start | bytes 688136 | tf_op jit(solution)/shard_map/ppermute | solution.py:24
  8.8 1.9 %collective-permute-start.1 = (f32[10,32,128]{2,1,0:T(8,128)S(1)}, f32[10,32,128]{2,1,0:T(8,128)S(1)}, u32[]{:S(2)}, u32[]{:S(2)}) collective-permute-start(f32[10,32,128]{2,1,0:T(8,128)S(1)} %get-tuple-element.11), channel_id=1, source_target_pairs={{1,0},{2,1},{3,2},{4,3},{5,4},{6,5},{7,6},{8,7},{9,8},{10,9},{11,1... | collective-permute-start | bytes 491528 | tf_op jit(solution)/shard_map/ppermute | solution.py:24
  10.7 4.7 %collective-permute-done.1.down_ref = f32[10,32,128]{2,1,0:T(8,128)S(1)} collective-permute-done((f32[10,32,128]{2,1,0:T(8,128)S(1)}, f32[10,32,128]{2,1,0:T(8,128)S(1)}, u32[]{:S(2)}, u32[]{:S(2)}) %collective-permute-start.1) | collective-permute-done | bytes 163872 | tf_op jit(solution)/shard_map/ppermute | solution.py:24
  15.4 0.0 collective-permute-done.up_ref
  15.4 0.0 copy-start.6
  15.5 5.6 %collective-permute-start.3 = (f32[10,24,128]{2,1,0:T(8,128)S(1)}, f32[10,24,128]{2,1,0:T(8,128)S(1)}, u32[]{:S(2)}, u32[]{:S(2)}) collective-permute-start(f32[10,24,128]{2,1,0:T(8,128)S(1)} %get-tuple-element.13), channel_id=1, source_target_pairs={{16,0},{32,16},{48,32},{64,48},{80,64},{96,80},{112,96},{128,112},... | collective-permute-start | bytes 368648 | tf_op jit(solution)/shard_map/ppermute | solution.py:24
  21.1 1.9 %collective-permute-start.2 = (f32[14,24,128]{2,1,0:T(8,128)S(1)}, f32[14,24,128]{2,1,0:T(8,128)S(1)}, u32[]{:S(2)}, u32[]{:S(2)}) collective-permute-start(f32[14,24,128]{2,1,0:T(8,128)S(1)} %get-tuple-element.12), channel_id=1, source_target_pairs={{0,16},{16,32},{32,48},{48,64},{64,80},{80,96},{96,112},{112,128},... | collective-permute-start | bytes 516104 | tf_op jit(solution)/shard_map/ppermute | solution.py:24
  23.0 0.0 copy-done.6
  23.0 0.1 multiply_cosine_fusion
  23.1 0.1 pad_maximum_fusion.coef_ref
  23.2 0.0 collective-permute-done.3.left_ref
  23.2 7.3 %collective-permute-done.2.right_ref = f32[14,24,128]{2,1,0:T(8,128)S(1)} collective-permute-done((f32[14,24,128]{2,1,0:T(8,128)S(1)}, f32[14,24,128]{2,1,0:T(8,128)S(1)}, u32[]{:S(2)}, u32[]{:S(2)}) %collective-permute-start.2) | collective-permute-done | bytes 172064 | tf_op jit(solution)/shard_map/ppermute | solution.py:24
  30.5 0.0 copy-done.4
  30.5 0.0 copy-done.5
  30.5 6.1 %shard_map.96 = (f32[3,32,16,128]{3,2,1,0:T(8,128)}, f32[3,32,16,128]{3,2,1,0:T(8,128)}, f32[16,8,128]{2,1,0:T(8,128)S(1)}) custom-call(f32[3,32,16,128]{3,2,1,0:T(8,128)S(1)} %copy-done, f32[3,32,16,128]{3,2,1,0:T(8,128)S(1)} %copy-done.1, s32[32,16,128]{2,1,0:T(8,128)S(1)} %copy-done.2, s32[32,16,128]{2,1,0:T(8,128)S(1)} %copy-done.3, ...), custom_call_target="tpu_custom_call" | custom-call | tf_op jit(solution)/shard_map/pallas_call | solution.py:235
  36.7 16.3 %all_to_all.5.got_ref = f32[16,8,128]{2,1,0:T(8,128)S(1)} all-to-all(f32[16,8,128]{2,1,0:T(8,128)S(1)} %get-tuple-element.16), channel_id=1, replica_groups=mesh['gx'=48,'gy'=16] {'gy'}, dimensions={0} | all-to-all | bytes 131072 | tf_op jit(solution)/shard_map/all_to_all | solution.py:245
  53.0 0.9 %shard_map.97 = f32[1,2,32,256]{3,2,1,0:T(8,128)} custom-call(f32[16,8,128]{2,1,0:T(8,128)S(1)} %all_to_all.5.got_ref), custom_call_target="tpu_custom_call" | custom-call | tf_op jit(solution)/shard_map/pallas_call | solution.py:246
  (6 shorter events, 0.1 us)
Async XLA Ops:
  0.6 1.1 %copy-start = (f32[3,32,16,128]{3,2,1,0:T(8,128)S(1)}, f32[3,32,16,128]{3,2,1,0:T(8,128)}, u32[]{:S(2)}) copy-start(f32[3,32,16,128]{3,2,1,0:T(8,128)} %e_ref.5) | copy-start | bytes 2359300
  1.8 1.1 %copy-start.1 = (f32[3,32,16,128]{3,2,1,0:T(8,128)S(1)}, f32[3,32,16,128]{3,2,1,0:T(8,128)}, u32[]{:S(2)}) copy-start(f32[3,32,16,128]{3,2,1,0:T(8,128)} %h_ref.5) | copy-start | bytes 2359300
  2.9 0.9 %copy-start.2 = (s32[32,16,128]{2,1,0:T(8,128)S(1)}, s32[32,16,128]{2,1,0:T(8,128)}, u32[]{:S(2)}) copy-start(s32[32,16,128]{2,1,0:T(8,128)} %m_ref.5) | copy-start | bytes 786436
  3.8 0.9 %copy-start.3 = (s32[32,16,128]{2,1,0:T(8,128)S(1)}, s32[32,16,128]{2,1,0:T(8,128)}, u32[]{:S(2)}) copy-start(s32[32,16,128]{2,1,0:T(8,128)} %p_ref.5) | copy-start | bytes 786436
  5.0 10.4 %collective-permute-start = (f32[14,32,128]{2,1,0:T(8,128)S(1)}, f32[14,32,128]{2,1,0:T(8,128)S(1)}, u32[]{:S(2)}, u32[]{:S(2)}) collective-permute-start(f32[14,32,128]{2,1,0:T(8,128)S(1)} %get-tuple-element.10), channel_id=1, source_target_pairs={{0,1},{1,2},{2,3},{3,4},{4,5},{5,6},{6,7},{7,8},{8,9},{9,10},{10,1... | collective-permute-start | bytes 688136 | tf_op jit(solution)/shard_map/ppermute | solution.py:24
  8.8 6.6 %collective-permute-start.1 = (f32[10,32,128]{2,1,0:T(8,128)S(1)}, f32[10,32,128]{2,1,0:T(8,128)S(1)}, u32[]{:S(2)}, u32[]{:S(2)}) collective-permute-start(f32[10,32,128]{2,1,0:T(8,128)S(1)} %get-tuple-element.11), channel_id=1, source_target_pairs={{1,0},{2,1},{3,2},{4,3},{5,4},{6,5},{7,6},{8,7},{9,8},{10,9},{11,1... | collective-permute-start | bytes 491528 | tf_op jit(solution)/shard_map/ppermute | solution.py:24
  15.4 7.5 %copy-start.6 = (f32[8]{0:T(128)S(1)}, f32[8]{0:T(128)}, u32[]{:S(2)}) copy-start(f32[8]{0:T(128)} %param.13) | copy-start | bytes 100
  15.5 7.7 %collective-permute-start.3 = (f32[10,24,128]{2,1,0:T(8,128)S(1)}, f32[10,24,128]{2,1,0:T(8,128)S(1)}, u32[]{:S(2)}, u32[]{:S(2)}) collective-permute-start(f32[10,24,128]{2,1,0:T(8,128)S(1)} %get-tuple-element.13), channel_id=1, source_target_pairs={{16,0},{32,16},{48,32},{64,48},{80,64},{96,80},{112,96},{128,112},... | collective-permute-start | bytes 368648 | tf_op jit(solution)/shard_map/ppermute | solution.py:24
  21.1 9.5 %collective-permute-start.2 = (f32[14,24,128]{2,1,0:T(8,128)S(1)}, f32[14,24,128]{2,1,0:T(8,128)S(1)}, u32[]{:S(2)}, u32[]{:S(2)}) collective-permute-start(f32[14,24,128]{2,1,0:T(8,128)S(1)} %get-tuple-element.12), channel_id=1, source_target_pairs={{0,16},{16,32},{32,48},{48,64},{64,80},{80,96},{96,112},{112,128},... | collective-permute-start | bytes 516104 | tf_op jit(solution)/shard_map/ppermute | solution.py:24
  23.2 7.3 %copy-start.4 = (f32[128]{0:T(128)S(1)}, f32[128]{0:T(128)}, u32[]{:S(2)}) copy-start(f32[128]{0:T(128)} %param.12) | copy-start | bytes 1540
  23.2 7.3 %copy-start.5 = (f32[4]{0:T(128)S(1)}, f32[4]{0:T(128)}, u32[]{:S(2)}) copy-start(f32[4]{0:T(128)} %eps_ref.1) | copy-start | bytes 52

commit v2 on v0

v2 whole, which is shorter than its diff:
```python
import jax
import jax.numpy as jnp
from jax import lax
from jax.experimental import pallas as pl
from jax.experimental.pallas import tpu as pltpu
from jax.sharding import PartitionSpec as P

STEPS = 2
NFREQ = 8
NMAT = 4
time_step = 0.5

EX, EY, EZ, HX, HY, HZ, FL, MT = range(8)
ALL = tuple(range(8))
U_MSG = tuple((-1, f) for f in ALL) + tuple((-2, f) for f in (EX, EY, EZ, HX, HZ, FL))
D_MSG = tuple((0, f) for f in ALL) + tuple((1, f) for f in (EX, EZ))
R_MSG = tuple((-1, f) for f in ALL) + tuple((-2, f) for f in (EX, EY, EZ, HY, HZ, FL))
L_MSG = tuple((0, f) for f in ALL) + tuple((1, f) for f in (EY, EZ))


MSG = len(U_MSG)


def paired(axis, first):
    devices = lax.axis_size(axis)
    return [(i, i + 1) for i in range(first, devices - 1, 2)]


def swap_outer(x, axis):
    pairs = paired(axis, 1)
    return lax.ppermute(x, axis, pairs + [(b, a) for a, b in pairs])


def gather_inner(x, axis):
    return lax.all_gather(x, axis, axis=0, axis_index_groups=[list(p) for p in paired(axis, 0)])


def is_second(axis):
    return lax.axis_index(axis) % 2


def field_plane(refs, f, x):
    e_ref, h_ref, code_ref = refs
    if f < 3:
        return e_ref[f, x]
    if f < 6:
        return h_ref[f - 3, x]
    return code_ref[f - FL, x]


def field_rows(refs, f, y):
    e_ref, h_ref, code_ref = refs
    ref, at = (e_ref, f) if f < 3 else (h_ref, f - 3) if f < 6 else (code_ref, f - FL)
    count, nx, ny = ref.shape[0], ref.shape[1], ref.shape[2]
    return ref.reshape(count * nx * ny, 128)[pl.ds(at * nx * ny + y, nx, stride=ny)]


def load_kernel(e_hbm, h_hbm, m_hbm, p_hbm, e_ref, h_ref, code_ref, inner_ref, outer_ref, m_ref, p_ref, sems):
    copies = [
        pltpu.make_async_copy(src, dst, sems.at[i])
        for i, (src, dst) in enumerate(((e_hbm, e_ref), (h_hbm, h_ref), (m_hbm, m_ref), (p_hbm, p_ref)))
    ]
    for copy in copies:
        copy.start()
    for copy in copies:
        copy.wait()
    code_ref[0] = p_ref[...].astype(jnp.float32) + 1.0
    code_ref[1] = m_ref[...].astype(jnp.float32) + 1.0
    refs = (e_ref, h_ref, code_ref)
    ny = m_ref.shape[1]

    def pack(up_ref, down_ref):
        for i, (at, f) in enumerate(U_MSG):
            up_ref[i] = field_rows(refs, f, ny + at)
        for i, (at, f) in enumerate(D_MSG):
            down_ref[i] = field_rows(refs, f, at)

    second = is_second("gy")

    @pl.when(second == 0)
    def _():
        pack(inner_ref, outer_ref)

    @pl.when(second == 1)
    def _():
        pack(outer_ref, inner_ref)


def planes_kernel(e_ref, h_ref, code_ref, inner_got, outer_got, inner_ref, outer_ref, third_ref):
    refs = (e_ref, h_ref, code_ref)
    nx = e_ref.shape[1]
    flat = third_ref.reshape(8 * nx * 8, 128)

    def fill(up_ref, down_ref):
        for i, (at, f) in enumerate(U_MSG):
            flat[pl.ds(f * nx * 8 + 8 + at, nx, stride=8)] = up_ref[i]
        for i, (at, f) in enumerate(D_MSG):
            flat[pl.ds(f * nx * 8 + at, nx, stride=8)] = down_ref[i]

    second = is_second("gy")

    @pl.when(second == 0)
    def _():
        fill(outer_got, inner_got.at[1])

    @pl.when(second == 1)
    def _():
        fill(inner_got.at[0], outer_got)

    def pack(right_ref, left_ref):
        for message, ref, base in ((R_MSG, right_ref, nx), (L_MSG, left_ref, 0)):
            for i, (at, f) in enumerate(message):
                ref[i, 0:16] = field_plane(refs, f, base + at)
                ref[i, 16:24] = third_ref[f, base + at]

    second_x = is_second("gx")

    @pl.when(second_x == 0)
    def _():
        pack(inner_ref, outer_ref)

    @pl.when(second_x == 1)
    def _():
        pack(outer_ref, inner_ref)


def next_y(a):
    return pltpu.roll(a, a.shape[0] - 1, 0)


def last_y(a):
    return pltpu.roll(a, 1, 0)


class Window:
    def __init__(self, sigma_ref, eps_ref):
        rows = (24, 128)
        lane = lax.broadcasted_iota(jnp.int32, rows, 1)
        self.not_last = lane != 127
        self.not_first = lane != 0
        sigma = sigma_ref[...]
        s_mag = sigma * time_step / 2.0
        self.h_keep_row = jnp.broadcast_to((1.0 - s_mag) / (1.0 + s_mag), rows)
        self.h_gain_row = jnp.broadcast_to(time_step / (1.0 + s_mag), rows)
        self.e_keep_rows, self.e_gain_rows, self.e_gain_free = [], [], []
        for k in range(NMAT):
            eps = jnp.full((1, 128), eps_ref[k], jnp.float32)
            s_ele = sigma * time_step / (2.0 * eps)
            self.e_keep_rows.append(jnp.broadcast_to((1.0 - s_ele) / (1.0 + s_ele), rows))
            self.e_gain_rows.append(jnp.broadcast_to(time_step / (eps * (1.0 + s_ele)), rows))
            self.e_gain_free.append(jnp.broadcast_to(time_step / eps, rows))

    def next_z(self, a):
        return jnp.where(self.not_last[: a.shape[0]], pltpu.roll(a, 127, 1), 0.0)

    def last_z(self, a):
        return jnp.where(self.not_first[: a.shape[0]], pltpu.roll(a, 1, 1), 0.0)

    def h_coefs(self, flag):
        keep = jnp.where(flag == 2.0, self.h_keep_row, 1.0)
        gain = jnp.where(flag == 2.0, self.h_gain_row, jnp.where(flag == 0.0, 0.0, time_step))
        return keep, gain

    def e_coefs(self, flag, code):
        m1, m2, m3 = code == 1.0, code == 2.0, code == 3.0

        def pick(table):
            return jnp.where(m1, table[0], jnp.where(m2, table[1], jnp.where(m3, table[2], table[3])))

        keep = jnp.where(flag == 2.0, pick(self.e_keep_rows), 1.0)
        gain = jnp.where(flag == 2.0, pick(self.e_gain_rows), pick(self.e_gain_free))
        return keep, jnp.where(code == 0.0, 0.0, gain)

    def h_step(self, h, e, e_next, coefs, with_x):
        keep, gain = coefs
        ex, ey, ez = e
        hx = None
        if with_x:
            hx = keep * h[0] - gain * ((next_y(ez) - ez) - (self.next_z(ey) - ey))
        hy = keep * h[1] - gain * ((self.next_z(ex) - ex) - (e_next[2] - ez))
        hz = keep * h[2] - gain * ((e_next[1] - ey) - (next_y(ex) - ex))
        return hx, hy, hz

    def e_step(self, e, h, h_last, coefs, rows=24):
        keep, gain = [c[:rows] for c in coefs]
        hz_y, hx_y = last_y(h[2])[:rows], last_y(h[0])[:rows]
        hx, hy, hz = [a[:rows] for a in h]
        ex = keep * e[0][:rows] + gain * ((hz - hz_y) - (hy - self.last_z(hy)))
        ey = keep * e[1][:rows] + gain * ((hx - self.last_z(hx)) - (hz - h_last[2][:rows]))
        ez = keep * e[2][:rows] + gain * ((hy - h_last[1][:rows]) - (hx - hx_y))
        return ex, ey, ez

    def run(self, planes, first, last, keep_first_step, store, skew):
        e0, h0, hc, ec, h1, e1, h2 = {}, {}, {}, {}, {}, {}, {}

        def fetch(x):
            if x not in e0:
                p = planes(x)
                e0[x], h0[x] = p[:3], p[3:6]
                if x <= last:
                    hc[x] = self.h_coefs(p[FL])
                if first - 1 <= x <= last:
                    ec[x] = self.e_coefs(p[FL], p[MT])

        for turn in range(first - 2, last + 2 + 3 * skew):
            x = turn
            if x <= last:
                fetch(x)
                fetch(x + 1)
                h1[x] = self.h_step(h0[x], e0[x], e0[x + 1], hc[x], x > first - 2)
            x = turn - skew
            if first - 1 <= x <= last:
                e1[x] = self.e_step(e0[x], h1[x], h1[x - 1], ec[x])
                if first <= x < last:
                    keep_first_step(x, e1[x])
            x = turn - 2 * skew - 1
            if first - 1 <= x < last:
                h2[x] = self.h_step(h1[x], e1[x], e1[x + 1], hc[x], True)
            x = turn - 3 * skew - 1
            if first <= x < last:
                store(x, self.e_step(e1[x], h2[x], h2[x - 1], ec[x], 16), h2[x])


def plane_tile(fetch, xs):
    tile = (8, 128)
    lead = lax.broadcasted_iota(jnp.int32, tile, 1) - lax.broadcasted_iota(jnp.int32, tile, 0)
    row = lax.broadcasted_iota(jnp.int32, tile, 0)
    out = jnp.zeros(tile, jnp.float32)
    for low in range(8):
        total = jnp.zeros(tile, jnp.float32)
        here = [x for x in xs if x % 8 == low]
        if not here:
            continue
        for x in here:
            for c in range(2):
                for half in range(2):
                    value = jnp.broadcast_to(fetch(c, x, half)[:, 64:65], tile)
                    total = jnp.where(lead == (c * 4 + x // 8) * 16 + half * 8, value, total)
        out = jnp.where(row == low, jnp.sum(total, axis=0, keepdims=True), out)
    return out


def inner_kernel(e_ref, h_ref, code_ref, third_ref, sigma_ref, eps_ref, eo_ref, ho_ref, tile_ref, first_ref):
    refs = (e_ref, h_ref, code_ref)
    nx = e_ref.shape[1]

    def planes(x):
        return [jnp.concatenate([field_plane(refs, f, x), third_ref[f, x]], axis=0) for f in ALL]

    def keep_first_step(x, e):
        first_ref[0, x] = e[0][0:16]
        first_ref[1, x] = e[1][0:16]

    def store(x, e, h):
        for c in range(3):
            eo_ref[c, x] = e[c]
            ho_ref[c, x] = h[c][0:16]

    Window(sigma_ref, eps_ref).run(planes, 2, nx - 2, keep_first_step, store, SKEW)
    for step, ref in enumerate((first_ref, eo_ref)):
        tile_ref[step] = plane_tile(lambda c, x, half: ref[c, x, half * 8:half * 8 + 8, :], range(2, nx - 2))


def edge_kernel(e_ref, h_ref, code_ref, third_ref, inner_got, outer_got, sigma_ref, eps_ref, tile_ref, coef_ref,
                eo_ref, ho_ref, part_ref, first_ref, right_ref, left_ref):
    refs = (e_ref, h_ref, code_ref)
    nx = e_ref.shape[1]
    second = is_second("gx")

    @pl.when(second == 0)
    def _():
        right_ref[...] = outer_got[...]
        left_ref[...] = inner_got[1]

    @pl.when(second == 1)
    def _():
        right_ref[...] = inner_got[0]
        left_ref[...] = outer_got[...]

    def planes(x):
        if 0 <= x < nx:
            return [jnp.concatenate([field_plane(refs, f, x), third_ref[f, x]], axis=0) for f in ALL]
        message, ref, at = (R_MSG, right_ref, x) if x < 0 else (L_MSG, left_ref, x - nx)
        return [ref[message.index((at, f))] if (at, f) in message else None for f in ALL]

    def slot(x):
        return x if x < 2 else x - nx + 4

    def keep_first_step(x, e):
        first_ref[0, slot(x)] = e[0][0:16]
        first_ref[1, slot(x)] = e[1][0:16]

    def store(x, e, h):
        for c in range(3):
            eo_ref[c, slot(x)] = e[c]
            ho_ref[c, slot(x)] = h[c][0:16]

    window = Window(sigma_ref, eps_ref)
    window.run(planes, 0, 2, keep_first_step, store, SKEW)
    window.run(planes, nx - 2, nx, keep_first_step, store, SKEW)
    tiles = []
    for step, ref in enumerate((first_ref, eo_ref)):
        edge = plane_tile(lambda c, x, half: ref[c, slot(x), half * 8:half * 8 + 8, :], (0, 1, nx - 2, nx - 1))
        tiles.append(tile_ref[step] + edge)
    for s in range(2 * NFREQ):
        part_ref[s] = coef_ref[0, s] * tiles[0] + coef_ref[1, s] * tiles[1]


def store_kernel(ei_ref, hi_ref, ee_ref, he_ref, eo_hbm, ho_hbm, sems):
    nx = ei_ref.shape[1]
    copies = []
    for inner, edge, out in ((ei_ref, ee_ref, eo_hbm), (hi_ref, he_ref, ho_hbm)):
        copies.append((inner.at[:, 2:nx - 2], out.at[:, 2:nx - 2]))
        copies.append((edge.at[:, 0:2], out.at[:, 0:2]))
        copies.append((edge.at[:, 2:4], out.at[:, nx - 2:nx]))
    copies = [pltpu.make_async_copy(src, dst, sems.at[i]) for i, (src, dst) in enumerate(copies)]
    for copy in copies:
        copy.start()
    for copy in copies:
        copy.wait()


def spectra_kernel(got_ref, out_ref):
    block = lax.broadcasted_iota(jnp.int32, (8, 128), 1) // 16
    for half in range(2):
        v = [got_ref[half * 8 + k] for k in range(8)]
        for bit in range(3):
            by = 1 << bit
            low_block = (block // by) % 2 == 0
            for a in range(8):
                if a & by:
                    continue
                low, high = v[a], v[a + by]
                v[a] = jnp.where(low_block, low, pltpu.roll(high, 16 * by, 1))
                v[a + by] = jnp.where(low_block, pltpu.roll(low, 128 - 16 * by, 1), high)
        for j in range(8):
            out_ref[0, j // 4, (j % 4) * 8:(j % 4) * 8 + 8, half * 128:half * 128 + 128] = v[j]


def shape(*dims):
    return jax.ShapeDtypeStruct(dims, jnp.float32)


SKEW = 1
VM = pl.BlockSpec(memory_space=pltpu.VMEM)
SM = pl.BlockSpec(memory_space=pltpu.SMEM)
HBM = pl.BlockSpec(memory_space=pltpu.HBM)
LIMIT = pltpu.CompilerParams(vmem_limit_bytes=16 << 20)


def cost(flops):
    return pl.CostEstimate(flops=flops, bytes_accessed=4 << 20, transcendentals=0)


def local(electric, magnetic, material, pml_flags, permittivity, pml_sigma, omega):
    nx, ny, nz = material.shape
    moments = jnp.arange(1, STEPS + 1, dtype=jnp.float32)[:, None] * time_step
    coef = jnp.concatenate([jnp.cos(omega[None] * moments), -jnp.sin(omega[None] * moments)], axis=1)
    whole, edge = shape(3, nx, ny, nz), shape(3, 4, ny, nz)

    e, h, code, inner, outer = pl.pallas_call(
        load_kernel,
        out_shape=(whole, whole, shape(2, nx, ny, nz), shape(MSG, nx, nz), shape(MSG, nx, nz)),
        in_specs=[HBM] * 4, out_specs=(VM,) * 5,
        scratch_shapes=[
            pltpu.VMEM((nx, ny, nz), jnp.int32), pltpu.VMEM((nx, ny, nz), jnp.int32), pltpu.SemaphoreType.DMA((4,)),
        ], compiler_params=LIMIT,
    )(*(pltpu.with_memory_space_constraint(a, pltpu.HBM) for a in (electric, magnetic, material, pml_flags)))
    outer, inner = swap_outer(outer, "gy"), gather_inner(inner, "gy")
    inner, outer, third = pl.pallas_call(
        planes_kernel,
        out_shape=(shape(MSG, 24, nz), shape(MSG, 24, nz), shape(8, nx, 8, nz)),
        in_specs=[VM] * 5, out_specs=(VM,) * 3, compiler_params=LIMIT,
    )(e, h, code, inner, outer)
    outer, inner = swap_outer(outer, "gx"), gather_inner(inner, "gx")
    sigma = pml_sigma[None]
    ei, hi, tile = pl.pallas_call(
        inner_kernel,
        out_shape=(whole, whole, shape(2, 8, 128)),
        in_specs=[VM] * 5 + [SM], out_specs=(VM,) * 3,
        scratch_shapes=[pltpu.VMEM((2, nx, ny, nz), jnp.float32)], compiler_params=LIMIT,
        cost_estimate=cost(40 << 20),
    )(e, h, code, third, sigma, permittivity)
    ee, he, part = pl.pallas_call(
        edge_kernel,
        out_shape=(edge, edge, shape(2 * NFREQ, 8, 128)),
        in_specs=[VM] * 7 + [SM, VM, SM], out_specs=(VM,) * 3,
        scratch_shapes=[
            pltpu.VMEM((2, 4, ny, nz), jnp.float32),
            pltpu.VMEM((MSG, 24, nz), jnp.float32), pltpu.VMEM((MSG, 24, nz), jnp.float32),
        ], compiler_params=LIMIT,
    )(e, h, code, third, inner, outer, sigma, permittivity, tile, coef)
    got = lax.all_to_all(part, "gy", split_axis=0, concat_axis=0, tiled=True)
    electric_out, magnetic_out = pl.pallas_call(
        store_kernel,
        out_shape=(whole, whole),
        in_specs=[VM] * 4, out_specs=(HBM, HBM),
        scratch_shapes=[pltpu.SemaphoreType.DMA((6,))], compiler_params=LIMIT,
        cost_estimate=cost(4 << 20),
    )(ei, hi, ee, he)
    spectra = pl.pallas_call(
        spectra_kernel,
        out_shape=shape(1, 2, nx, 16 * ny),
        in_specs=[VM], out_specs=VM, compiler_params=LIMIT,
    )(got)
    return electric_out, magnetic_out, spectra


def solution(mesh):
    placed = (
        P(None, "gx", "gy", None),
        P(None, "gx", "gy", None),
        P("gx", "gy", None),
        P("gx", "gy", None),
        P(),
        P(),
        P(),
    )
    return jax.shard_map(
        local,
        mesh=mesh,
        in_specs=placed,
        out_specs=(P(None, "gx", "gy", None), P(None, "gx", "gy", None), P("gy", None, "gx", None)),
        check_vma=False,
    )
```

time: 76.7 us -> 44.6 us (0.58)
  the two profiles are of different devices: /device:TPU:455 before, /device:TPU:513 now
where the time goes in v2:
time: 44.6 us; the launch traced here: 44.4 us
  starting transfers between devices  17.6 us (39%)
  blocking collectives  9.09 us (20%)
  Pallas kernels  8.04 us (18%)
  waiting for transfers between devices  7.42 us (17%)
  local copies, waits for them, and re-layouts  1.32 us (3%)
  between operations  0.68 us (2%)
    ppermute x2, starting transfers between devices, swap_outer(): return lax.ppermute(x, axis, pairs + [(b, a) for a, b in pairs])  9.35 us
    all_gather x2, blocking collectives, gather_inner(): lax.all_gather(x, axis, axis=0, axis_index_groups=[list(p) for p in paire...  9.09 us
    all_to_all x1, starting transfers between devices, local(): got = lax.all_to_all(part, 'gy', split_axis=0, concat_axis=0, tiled=True)  8.29 us
    all_to_all x1, waiting for transfers between devices, local(): got = lax.all_to_all(part, 'gy', split_axis=0, concat_axis=0, tiled=True)  6.63 us
    pallas_call x1, Pallas kernels, local(): pl.pallas_call(inner_kernel, out_shape=(whole, whole, shape(2, 8, 128)),...  2.46 us
    pallas_call x1, Pallas kernels, local(): pl.pallas_call(load_kernel, out_shape=(whole, whole, shape(2, nx, ny, nz)...  1.74 us
    pallas_call x1, Pallas kernels, local(): pl.pallas_call(edge_kernel, out_shape=(edge, edge, shape(2 * NFREQ, 8, 12...  1.68 us
    unnamed x6, local copies, waits for them, and re-layouts  1.32 us
  transfers between devices with their start and end apart: 3, of which 2 were waited for; matrix products, arithmetic and copies ran while one was open for 0% of the time, Pallas kernels for 8%

profile of v2, /device:TPU:513, one launch (start us, length us, event | category | flops | bytes accessed | tf_op | source)
XLA Modules:
  0.0 44.4 jit_solution(9883337765680036768)
XLA Ops:
  0.6 1.7 %shard_map.94 = (f32[3,32,16,128]{3,2,1,0:T(8,128)S(1)}, f32[3,32,16,128]{3,2,1,0:T(8,128)S(1)}, f32[2,32,16,128]{3,2,1,0:T(8,128)S(1)}, f32[14,32,128]{2,1,0:T(8,128)S(1)}, f32[14,32,128]{2,1,0:T(8,128)S(1)}) custom-call(f32[3,32,16,128]{3,2,1,0:T(8,128)} %e_hbm.1, f32[3,32,16,128]{3,2,1,0:T(8,128)} %h_hbm.1, s32[32,16,128]{2,1,0:T(8,128)} %m_hbm.1, ...), custom_call_target="tpu_custom_call" | custom-call | tf_op jit(solution)/shard_map/pallas_call | solution.py:361
  2.4 3.8 %collective-permute-start = (f32[14,32,128]{2,1,0:T(8,128)S(1)}, f32[14,32,128]{2,1,0:T(8,128)S(1)}, u32[]{:S(2)}, u32[]{:S(2)}) collective-permute-start(f32[14,32,128]{2,1,0:T(8,128)S(1)} %get-tuple-element.23), channel_id=1, source_target_pairs={{1,2},{3,4},{5,6},{7,8},{9,10},{11,12},{13,14},{2,1},{4,3},{6,5},{... | collective-permute-start | bytes 688136 | tf_op jit(solution)/shard_map/ppermute | solution.py:31
  6.1 2.1 %all-gather = f32[28,32,128]{2,1,0:T(8,128)S(1)} all-gather(f32[14,32,128]{2,1,0:T(8,128)S(1)} %get-tuple-element.22), channel_id=2, replica_groups={{0,1},{2,3},{4,5},{6,7},{8,9},{10,11},{12,13},{14,15},{16,17},{18,19},{..., dimensions={0}, use_global_device_ids=true | all-gather | bytes 688128 | tf_op jit(solution)/shard_map/all_gather | solution.py:35
  8.3 0.0 copy-start.2
  8.3 0.6 %copy-done.2 = f32[8]{0:T(128)S(1)} copy-done((f32[8]{0:T(128)S(1)}, f32[8]{0:T(128)}, u32[]{:S(2)}) %copy-start.2) | copy-done | bytes 56
  8.9 0.1 multiply_cosine_fusion
  9.1 0.8 %collective-permute-done.outer_got = f32[14,32,128]{2,1,0:T(8,128)S(1)} collective-permute-done((f32[14,32,128]{2,1,0:T(8,128)S(1)}, f32[14,32,128]{2,1,0:T(8,128)S(1)}, u32[]{:S(2)}, u32[]{:S(2)}) %collective-permute-start) | collective-permute-done | bytes 229408 | tf_op jit(solution)/shard_map/ppermute | solution.py:31
  9.8 0.1 shard_map.95
  10.0 5.6 %collective-permute-start.1 = (f32[14,24,128]{2,1,0:T(8,128)S(1)}, f32[14,24,128]{2,1,0:T(8,128)S(1)}, u32[]{:S(2)}, u32[]{:S(2)}) collective-permute-start(f32[14,24,128]{2,1,0:T(8,128)S(1)} %get-tuple-element.28), channel_id=1, source_target_pairs={{16,32},{48,64},{80,96},{112,128},{144,160},{176,192},{208,224},{2... | collective-permute-start | bytes 516104 | tf_op jit(solution)/shard_map/ppermute | solution.py:31
  15.6 0.1 pad_maximum_fusion.coef_ref
  15.7 0.0 copy-start
  15.7 0.0 copy-start.1
  15.7 0.7 %copy-done = f32[128]{0:T(128)S(1)} copy-done((f32[128]{0:T(128)S(1)}, f32[128]{0:T(128)}, u32[]{:S(2)}) %copy-start) | copy-done | bytes 536
  16.3 0.0 copy-done.1
  16.3 2.5 %shard_map.96 = (f32[3,32,16,128]{3,2,1,0:T(8,128)S(1)}, f32[3,32,16,128]{3,2,1,0:T(8,128)S(1)}, f32[2,8,128]{2,1,0:T(8,128)S(1)}) custom-call(f32[3,32,16,128]{3,2,1,0:T(8,128)S(1)} %get-tuple-element.19.e_ref, f32[3,32,16,128]{3,2,1,0:T(8,128)S(1)} %get-tuple-element.20.h_ref, f32[2,32,16,128]{3,2,1,0:T(8,128)S(1)} %get-tuple-element.21.code_ref, ...), custom_call_target="tpu_custom_call" | custom-call | flops 41943040 | bytes 4194304 | tf_op jit(solution)/shard_map/pallas_call | solution.py:377
  18.8 7.0 %all-gather.1 = f32[28,24,128]{2,1,0:T(8,128)S(1)} all-gather(f32[14,24,128]{2,1,0:T(8,128)S(1)} %get-tuple-element.27), channel_id=3, replica_groups={{0,16},{32,48},{64,80},{96,112},{128,144},{160,176},{192,208},{224,240}..., dimensions={0}, use_global_device_ids=true | all-gather | bytes 516096 | tf_op jit(solution)/shard_map/all_gather | solution.py:35
  25.7 0.0 collective-permute-done.1.outer_got
  25.7 1.7 %shard_map.97 = (f32[3,4,16,128]{3,2,1,0:T(8,128)S(1)}, f32[3,4,16,128]{3,2,1,0:T(8,128)S(1)}, f32[16,8,128]{2,1,0:T(8,128)}) custom-call(f32[3,32,16,128]{3,2,1,0:T(8,128)S(1)} %get-tuple-element.19.e_ref, f32[3,32,16,128]{3,2,1,0:T(8,128)S(1)} %get-tuple-element.20.h_ref, f32[2,32,16,128]{3,2,1,0:T(8,128)S(1)} %get-tuple-element.21.code_ref, ...), custom_call_target="tpu_custom_call" | custom-call | tf_op jit(solution)/shard_map/pallas_call | solution.py:384
  27.4 8.3 %all-to-all-start = ((f32[16,8,128]{2,1,0:T(8,128)}), f32[16,8,128]{2,1,0:T(8,128)S(1)}, u32[]{:S(2)}, u32[]{:S(2)}) async-start(f32[16,8,128]{2,1,0:T(8,128)} %get-tuple-element.34), calls=%async_computation | async-start | bytes 131072 | tf_op jit(solution)/shard_map/all_to_all | solution.py:393
  35.7 1.2 %shard_map.98 = (f32[3,32,16,128]{3,2,1,0:T(8,128)}, f32[3,32,16,128]{3,2,1,0:T(8,128)}) custom-call(f32[3,32,16,128]{3,2,1,0:T(8,128)S(1)} %get-tuple-element.25.ei_ref, f32[3,32,16,128]{3,2,1,0:T(8,128)S(1)} %get-tuple-element.26.hi_ref, f32[3,4,16,128]{3,2,1,0:T(8,128)S(1)} %get-tuple-element.30.ee_ref, f32[3,4,16,128]{3,2,1,0:T(8,128)S(1)} %get-tuple-element.31.he_ref), custom_call_target="tpu_custom_call" | custom-call | flops 4194304 | bytes 4194304 | tf_op jit(solution)/shard_map/pallas_call | solution.py:394
  36.9 6.6 %all-to-all-done.got_ref = f32[16,8,128]{2,1,0:T(8,128)S(1)} async-done(((f32[16,8,128]{2,1,0:T(8,128)}), f32[16,8,128]{2,1,0:T(8,128)S(1)}, u32[]{:S(2)}, u32[]{:S(2)}) %all-to-all-start) | async-done | bytes 65568 | tf_op jit(solution)/shard_map/all_to_all | solution.py:393
  43.5 0.9 %shard_map.99 = f32[1,2,32,256]{3,2,1,0:T(8,128)} custom-call(f32[16,8,128]{2,1,0:T(8,128)S(1)} %all-to-all-done.got_ref), custom_call_target="tpu_custom_call" | custom-call | tf_op jit(solution)/shard_map/pallas_call | solution.py:401
  (1 shorter events, 0.0 us)
Async XLA Ops:
  2.4 7.5 %collective-permute-start = (f32[14,32,128]{2,1,0:T(8,128)S(1)}, f32[14,32,128]{2,1,0:T(8,128)S(1)}, u32[]{:S(2)}, u32[]{:S(2)}) collective-permute-start(f32[14,32,128]{2,1,0:T(8,128)S(1)} %get-tuple-element.23), channel_id=1, source_target_pairs={{1,2},{3,4},{5,6},{7,8},{9,10},{11,12},{13,14},{2,1},{4,3},{6,5},{... | collective-permute-start | bytes 688136 | tf_op jit(solution)/shard_map/ppermute | solution.py:31
  8.3 0.7 %copy-start.2 = (f32[8]{0:T(128)S(1)}, f32[8]{0:T(128)}, u32[]{:S(2)}) copy-start(f32[8]{0:T(128)} %param.13) | copy-start | bytes 100
  10.0 15.8 %collective-permute-start.1 = (f32[14,24,128]{2,1,0:T(8,128)S(1)}, f32[14,24,128]{2,1,0:T(8,128)S(1)}, u32[]{:S(2)}, u32[]{:S(2)}) collective-permute-start(f32[14,24,128]{2,1,0:T(8,128)S(1)} %get-tuple-element.28), channel_id=1, source_target_pairs={{16,32},{48,64},{80,96},{112,128},{144,160},{176,192},{208,224},{2... | collective-permute-start | bytes 516104 | tf_op jit(solution)/shard_map/ppermute | solution.py:31
  15.7 0.7 %copy-start = (f32[128]{0:T(128)S(1)}, f32[128]{0:T(128)}, u32[]{:S(2)}) copy-start(f32[128]{0:T(128)} %param.12) | copy-start | bytes 1540
  15.7 0.7 %copy-start.1 = (f32[4]{0:T(128)S(1)}, f32[4]{0:T(128)}, u32[]{:S(2)}) copy-start(f32[4]{0:T(128)} %eps_ref.3) | copy-start | bytes 52
  27.4 16.1 %all-to-all-start = ((f32[16,8,128]{2,1,0:T(8,128)}), f32[16,8,128]{2,1,0:T(8,128)S(1)}, u32[]{:S(2)}, u32[]{:S(2)}) async-start(f32[16,8,128]{2,1,0:T(8,128)} %get-tuple-element.34), calls=%async_computation | async-start | bytes 131072 | tf_op jit(solution)/shard_map/all_to_all | solution.py:393

commit v3 on v2

--- a/solution.py
+++ b/solution.py
@@ -26,8 +26,8 @@
     return [(i, i + 1) for i in range(first, devices - 1, 2)]
 
 
-def swap_outer(x, axis):
-    pairs = paired(axis, 1)
+def swapped(x, axis, first):
+    pairs = paired(axis, first)
     return lax.ppermute(x, axis, pairs + [(b, a) for a, b in pairs])
 
 
@@ -55,15 +55,25 @@
     return ref.reshape(count * nx * ny, 128)[pl.ds(at * nx * ny + y, nx, stride=ny)]
 
 
-def load_kernel(e_hbm, h_hbm, m_hbm, p_hbm, e_ref, h_ref, code_ref, inner_ref, outer_ref, m_ref, p_ref, sems):
-    copies = [
-        pltpu.make_async_copy(src, dst, sems.at[i])
-        for i, (src, dst) in enumerate(((e_hbm, e_ref), (h_hbm, h_ref), (m_hbm, m_ref), (p_hbm, p_ref)))
-    ]
+def load_kernel(e_hbm, h_hbm, m_hbm, p_hbm, eps_hbm, sigma_hbm, omega_hbm,
+                e_ref, h_ref, code_ref, inner_ref, outer_ref, table_ref, omega_ref, m_ref, p_ref, sigma_ref, eps_ref, sems):
+    pairs = [(e_hbm.at[c], e_ref.at[c]) for c in range(3)] + [(h_hbm.at[c], h_ref.at[c]) for c in range(3)]
+    pairs += [(m_hbm, m_ref), (p_hbm, p_ref), (eps_hbm, eps_ref), (sigma_hbm, sigma_ref), (omega_hbm, omega_ref)]
+    copies = [pltpu.make_async_copy(src, dst, sems.at[i]) for i, (src, dst) in enumerate(pairs)]
     for copy in copies:
         copy.start()
     for copy in copies:
         copy.wait()
+    sigma = sigma_ref[...]
+    s_mag = sigma * time_step / 2.0
+    table_ref[0:1] = (1.0 - s_mag) / (1.0 + s_mag)
+    table_ref[1:2] = time_step / (1.0 + s_mag)
+    for k in range(NMAT):
+        eps = jnp.full((1, 128), eps_ref[k], jnp.float32)
+        s_ele = sigma * time_step / (2.0 * eps)
+        table_ref[2 + k:3 + k] = (1.0 - s_ele) / (1.0 + s_ele)
+        table_ref[6 + k:7 + k] = time_step / (eps * (1.0 + s_ele))
+        table_ref[10 + k:11 + k] = time_step / eps
     code_ref[0] = p_ref[...].astype(jnp.float32) + 1.0
     code_ref[1] = m_ref[...].astype(jnp.float32) + 1.0
     refs = (e_ref, h_ref, code_ref)
@@ -133,22 +143,14 @@
 
 
 class Window:
-    def __init__(self, sigma_ref, eps_ref):
+    def __init__(self, table_ref):
         rows = (24, 128)
         lane = lax.broadcasted_iota(jnp.int32, rows, 1)
         self.not_last = lane != 127
         self.not_first = lane != 0
-        sigma = sigma_ref[...]
-        s_mag = sigma * time_step / 2.0
-        self.h_keep_row = jnp.broadcast_to((1.0 - s_mag) / (1.0 + s_mag), rows)
-        self.h_gain_row = jnp.broadcast_to(time_step / (1.0 + s_mag), rows)
-        self.e_keep_rows, self.e_gain_rows, self.e_gain_free = [], [], []
-        for k in range(NMAT):
-            eps = jnp.full((1, 128), eps_ref[k], jnp.float32)
-            s_ele = sigma * time_step / (2.0 * eps)
-            self.e_keep_rows.append(jnp.broadcast_to((1.0 - s_ele) / (1.0 + s_ele), rows))
-            self.e_gain_rows.append(jnp.broadcast_to(time_step / (eps * (1.0 + s_ele)), rows))
-            self.e_gain_free.append(jnp.broadcast_to(time_step / eps, rows))
+        table = [jnp.broadcast_to(table_ref[k:k + 1], rows) for k in range(14)]
+        self.h_keep_row, self.h_gain_row = table[:2]
+        self.e_keep_rows, self.e_gain_rows, self.e_gain_free = table[2:6], table[6:10], table[10:14]
 
     def next_z(self, a):
         return jnp.where(self.not_last[: a.shape[0]], pltpu.roll(a, 127, 1), 0.0)
@@ -219,6 +221,7 @@
             x = turn - 3 * skew - 1
             if first <= x < last:
                 store(x, self.e_step(e1[x], h2[x], h2[x - 1], ec[x], 16), h2[x])
+            yield turn
 
 
 def plane_tile(fetch, xs):
@@ -240,7 +243,7 @@
     return out
 
 
-def inner_kernel(e_ref, h_ref, code_ref, third_ref, sigma_ref, eps_ref, eo_ref, ho_ref, tile_ref, first_ref):
+def inner_kernel(e_ref, h_ref, code_ref, third_ref, table_ref, eo_hbm, ho_hbm, tile_ref, first_ref, eo_ref, ho_ref, sems):
     refs = (e_ref, h_ref, code_ref)
     nx = e_ref.shape[1]
 
@@ -250,18 +253,29 @@
     def keep_first_step(x, e):
         first_ref[0, x] = e[0][0:16]
         first_ref[1, x] = e[1][0:16]
+
+    copies = []
 
     def store(x, e, h):
         for c in range(3):
             eo_ref[c, x] = e[c]
             ho_ref[c, x] = h[c][0:16]
-
-    Window(sigma_ref, eps_ref).run(planes, 2, nx - 2, keep_first_step, store, SKEW)
+        if x + 1 in CUTS:
+            start = 2 if x + 1 == CUTS[0] else CUTS[CUTS.index(x + 1) - 1]
+            for ref, hbm in ((eo_ref, eo_hbm), (ho_ref, ho_hbm)):
+                part = pl.ds(start, x + 1 - start)
+                copies.append(pltpu.make_async_copy(ref.at[:, part], hbm.at[:, part], sems.at[len(copies)]))
+                copies[-1].start()
+
+    for _ in Window(table_ref).run(planes, 2, nx - 2, keep_first_step, store, SKEW):
+        pass
     for step, ref in enumerate((first_ref, eo_ref)):
         tile_ref[step] = plane_tile(lambda c, x, half: ref[c, x, half * 8:half * 8 + 8, :], range(2, nx - 2))
-
-
-def edge_kernel(e_ref, h_ref, code_ref, third_ref, inner_got, outer_got, sigma_ref, eps_ref, tile_ref, coef_ref,
+    for copy in copies:
+        copy.wait()
+
+
+def edge_kernel(e_ref, h_ref, code_ref, third_ref, inner_got, outer_got, table_ref, tile_ref, coef_ref,
                 eo_ref, ho_ref, part_ref, first_ref, right_ref, left_ref):
     refs = (e_ref, h_ref, code_ref)
     nx = e_ref.shape[1]
@@ -270,11 +284,11 @@
     @pl.when(second == 0)
     def _():
         right_ref[...] = outer_got[...]
-        left_ref[...] = inner_got[1]
+        left_ref[...] = inner_got[...]
 
     @pl.when(second == 1)
     def _():
-        right_ref[...] = inner_got[0]
+        right_ref[...] = inner_got[...]
         left_ref[...] = outer_got[...]
 
     def planes(x):
@@ -295,9 +309,9 @@
             eo_ref[c, slot(x)] = e[c]
             ho_ref[c, slot(x)] = h[c][0:16]
 
-    window = Window(sigma_ref, eps_ref)
-    window.run(planes, 0, 2, keep_first_step, store, SKEW)
-    window.run(planes, nx - 2, nx, keep_first_step, store, SKEW)
+    window = Window(table_ref)
+    for _ in zip(*(window.run(planes, at, at + 2, keep_first_step, store, EDGE_SKEW) for at in (0, nx - 2))):
+        pass
     tiles = []
     for step, ref in enumerate((first_ref, eo_ref)):
         edge = plane_tile(lambda c, x, half: ref[c, slot(x), half * 8:half * 8 + 8, :], (0, 1, nx - 2, nx - 1))
@@ -306,21 +320,23 @@
         part_ref[s] = coef_ref[0, s] * tiles[0] + coef_ref[1, s] * tiles[1]
 
 
-def store_kernel(ei_ref, hi_ref, ee_ref, he_ref, eo_hbm, ho_hbm, sems):
-    nx = ei_ref.shape[1]
-    copies = []
-    for inner, edge, out in ((ei_ref, ee_ref, eo_hbm), (hi_ref, he_ref, ho_hbm)):
-        copies.append((inner.at[:, 2:nx - 2], out.at[:, 2:nx - 2]))
-        copies.append((edge.at[:, 0:2], out.at[:, 0:2]))
-        copies.append((edge.at[:, 2:4], out.at[:, nx - 2:nx]))
-    copies = [pltpu.make_async_copy(src, dst, sems.at[i]) for i, (src, dst) in enumerate(copies)]
+def last_kernel(got_ref, ee_ref, he_ref, _e, _h, eo_hbm, ho_hbm, spectra_hbm, out_ref, sems):
+    nx = eo_hbm.shape[1]
+    pairs = []
+    for edge, out in ((ee_ref, eo_hbm), (he_ref, ho_hbm)):
+        pairs.append((edge.at[:, 0:2], out.at[:, 0:2]))
+        pairs.append((edge.at[:, 2:4], out.at[:, nx - 2:nx]))
+    copies = [pltpu.make_async_copy(src, dst, sems.at[i]) for i, (src, dst) in enumerate(pairs)]
     for copy in copies:
         copy.start()
+    unpack(got_ref, out_ref)
+    copies.append(pltpu.make_async_copy(out_ref, spectra_hbm, sems.at[len(pairs)]))
+    copies[-1].start()
     for copy in copies:
         copy.wait()
 
 
-def spectra_kernel(got_ref, out_ref):
+def unpack(got_ref, out_ref):
     block = lax.broadcasted_iota(jnp.int32, (8, 128), 1) // 16
     for half in range(2):
         v = [got_ref[half * 8 + k] for k in range(8)]
@@ -342,6 +358,8 @@
 
 
 SKEW = 1
+EDGE_SKEW = 1
+CUTS = (10, 18, 26, 30)
 VM = pl.BlockSpec(memory_space=pltpu.VMEM)
 SM = pl.BlockSpec(memory_space=pltpu.SMEM)
 HBM = pl.BlockSpec(memory_space=pltpu.HBM)
@@ -355,54 +373,51 @@
 def local(electric, magnetic, material, pml_flags, permittivity, pml_sigma, omega):
     nx, ny, nz = material.shape
     moments = jnp.arange(1, STEPS + 1, dtype=jnp.float32)[:, None] * time_step
-    coef = jnp.concatenate([jnp.cos(omega[None] * moments), -jnp.sin(omega[None] * moments)], axis=1)
     whole, edge = shape(3, nx, ny, nz), shape(3, 4, ny, nz)
 
-    e, h, code, inner, outer = pl.pallas_call(
+    e, h, code, inner, outer, table, omega = pl.pallas_call(
         load_kernel,
-        out_shape=(whole, whole, shape(2, nx, ny, nz), shape(MSG, nx, nz), shape(MSG, nx, nz)),
-        in_specs=[HBM] * 4, out_specs=(VM,) * 5,
+        out_shape=(whole, whole, shape(2, nx, ny, nz), shape(MSG, nx, nz), shape(MSG, nx, nz), shape(16, nz), shape(1, NFREQ)),
+        in_specs=[HBM] * 7, out_specs=(VM,) * 7,
         scratch_shapes=[
-            pltpu.VMEM((nx, ny, nz), jnp.int32), pltpu.VMEM((nx, ny, nz), jnp.int32), pltpu.SemaphoreType.DMA((4,)),
+            pltpu.VMEM((nx, ny, nz), jnp.int32), pltpu.VMEM((nx, ny, nz), jnp.int32),
+            pltpu.VMEM((1, nz), jnp.float32), pltpu.SMEM((NMAT,), jnp.float32), pltpu.SemaphoreType.DMA((11,)),
         ], compiler_params=LIMIT,
-    )(*(pltpu.with_memory_space_constraint(a, pltpu.HBM) for a in (electric, magnetic, material, pml_flags)))
-    outer, inner = swap_outer(outer, "gy"), gather_inner(inner, "gy")
+    )(*(pltpu.with_memory_space_constraint(a, pltpu.HBM) for a in (
+        electric, magnetic, material, pml_flags, permittivity, pml_sigma[None], omega[None])))
+    coef = jnp.concatenate([jnp.cos(omega * moments), -jnp.sin(omega * moments)], axis=1)
+    outer, inner = swapped(outer, "gy", 1), gather_inner(inner, "gy")
     inner, outer, third = pl.pallas_call(
         planes_kernel,
         out_shape=(shape(MSG, 24, nz), shape(MSG, 24, nz), shape(8, nx, 8, nz)),
         in_specs=[VM] * 5, out_specs=(VM,) * 3, compiler_params=LIMIT,
     )(e, h, code, inner, outer)
-    outer, inner = swap_outer(outer, "gx"), gather_inner(inner, "gx")
-    sigma = pml_sigma[None]
+    outer, inner = swapped(outer, "gx", 1), swapped(inner, "gx", 0)
     ei, hi, tile = pl.pallas_call(
         inner_kernel,
         out_shape=(whole, whole, shape(2, 8, 128)),
-        in_specs=[VM] * 5 + [SM], out_specs=(VM,) * 3,
-        scratch_shapes=[pltpu.VMEM((2, nx, ny, nz), jnp.float32)], compiler_params=LIMIT,
-        cost_estimate=cost(40 << 20),
-    )(e, h, code, third, sigma, permittivity)
+        in_specs=[VM] * 5, out_specs=(HBM, HBM, VM),
+        scratch_shapes=[
+            pltpu.VMEM((2, nx, ny, nz), jnp.float32), pltpu.VMEM((3, nx, ny, nz), jnp.float32),
+            pltpu.VMEM((3, nx, ny, nz), jnp.float32), pltpu.SemaphoreType.DMA((2 * len(CUTS),)),
+        ], compiler_params=LIMIT, cost_estimate=cost(40 << 20),
+    )(e, h, code, third, table)
     ee, he, part = pl.pallas_call(
         edge_kernel,
         out_shape=(edge, edge, shape(2 * NFREQ, 8, 128)),
-        in_specs=[VM] * 7 + [SM, VM, SM], out_specs=(VM,) * 3,
+        in_specs=[VM] * 8 + [SM], out_specs=(VM,) * 3,
         scratch_shapes=[
             pltpu.VMEM((2, 4, ny, nz), jnp.float32),
             pltpu.VMEM((MSG, 24, nz), jnp.float32), pltpu.VMEM((MSG, 24, nz), jnp.float32),
         ], compiler_params=LIMIT,
-    )(e, h, code, third, inner, outer, sigma, permittivity, tile, coef)
+    )(e, h, code, third, inner, outer, table, tile, coef)
     got = lax.all_to_all(part, "gy", split_axis=0, concat_axis=0, tiled=True)
-    electric_out, magnetic_out = pl.pallas_call(
-        store_kernel,
-        out_shape=(whole, whole),
-        in_specs=[VM] * 4, out_specs=(HBM, HBM),
-        scratch_shapes=[pltpu.SemaphoreType.DMA((6,))], compiler_params=LIMIT,
-        cost_estimate=cost(4 << 20),
-    )(ei, hi, ee, he)
-    spectra = pl.pallas_call(
-        spectra_kernel,
-        out_shape=shape(1, 2, nx, 16 * ny),
-        in_specs=[VM], out_specs=VM, compiler_params=LIMIT,
-    )(got)
+    electric_out, magnetic_out, spectra = pl.pallas_call(
+        last_kernel,
+        out_shape=(whole, whole, shape(1, 2, nx, 16 * ny)),
+        in_specs=[VM] * 3 + [HBM] * 2, out_specs=(HBM,) * 3, input_output_aliases={3: 0, 4: 1},
+        scratch_shapes=[pltpu.VMEM((1, 2, nx, 16 * ny), jnp.float32), pltpu.SemaphoreType.DMA((5,))], compiler_params=LIMIT,
+    )(got, ee, he, ei, hi)
     return electric_out, magnetic_out, spectra
 
 

time: 44.6 us -> 42.7 us (0.957)
  blocking collectives: 9.09 us -> 18.9 us
  starting transfers between devices: 17.6 us -> 11.8 us
  waiting for transfers between devices: 7.42 us -> 4.65 us
  Pallas kernels: 8.04 us -> 6.28 us
  local copies, waits for them, and re-layouts: 1.32 us -> 0 us
    all_to_all x0 -> x1, blocking collectives: none -> 16.7 us  [local(): got = lax.all_to_all(part, 'gy', split_axis=0, concat_axis=0, tiled=True)]
    all_to_all x1 -> x0, starting transfers between devices: 8.29 us -> none  [local(): got = lax.all_to_all(part, 'gy', split_axis=0, concat_axis=0, tiled=True)]
    all_gather x2 -> x1, blocking collectives: 9.09 us -> 2.14 us  [gather_inner(): lax.all_gather(x, axis, axis=0, axis_index_groups=[list(p) for p in paire...]
    all_to_all x1 -> x0, waiting for transfers between devices: 6.63 us -> none  [local(): got = lax.all_to_all(part, 'gy', split_axis=0, concat_axis=0, tiled=True)]
    ppermute x2 -> x3, waiting for transfers between devices: 0.79 us -> 4.65 us  [swapped(): return lax.ppermute(x, axis, pairs + [(b, a) for a, b in pairs])]
    ppermute x2 -> x3, starting transfers between devices: 9.35 us -> 11.8 us  [swapped(): return lax.ppermute(x, axis, pairs + [(b, a) for a, b in pairs])]
    unnamed x6 -> x0, local copies, waits for them, and re-layouts: 1.32 us -> none
    pallas_call x2 -> x1, Pallas kernels: 2.03 us -> 0.9 us  [local(): pl.pallas_call(last_kernel, out_shape=(whole, whole, shape(1, 2, nx, 16 *...]
  transfers between devices with their start and end apart: 3 -> 3, of which waited for: 2 -> 2; matrix products, arithmetic and copies ran while one was open for 0% -> 0% of each run, Pallas kernels for 8% -> 6%
where the time goes in v3:
time: 42.7 us; the launch traced here: 42.5 us
  blocking collectives  18.9 us (44%)
  starting transfers between devices  11.8 us (28%)
  Pallas kernels  6.28 us (15%)
  waiting for transfers between devices  4.65 us (11%)
  between operations  0.7 us (2%)
    all_to_all x1, blocking collectives, local(): got = lax.all_to_all(part, 'gy', split_axis=0, concat_axis=0, tiled=True)  16.7 us
    ppermute x3, starting transfers between devices, swapped(): return lax.ppermute(x, axis, pairs + [(b, a) for a, b in pairs])  11.8 us
    ppermute x3, waiting for transfers between devices, swapped(): return lax.ppermute(x, axis, pairs + [(b, a) for a, b in pairs])  4.65 us
    pallas_call x1, Pallas kernels, local(): pl.pallas_call(inner_kernel, out_shape=(whole, whole, shape(2, 8, 128)),...  2.41 us
    all_gather x1, blocking collectives, gather_inner(): lax.all_gather(x, axis, axis=0, axis_index_groups=[list(p) for p in paire...  2.14 us
    pallas_call x1, Pallas kernels, local(): pl.pallas_call(load_kernel, out_shape=(whole, whole, shape(2, nx, ny, nz)...  1.82 us
    pallas_call x1, Pallas kernels, local(): pl.pallas_call(edge_kernel, out_shape=(edge, edge, shape(2 * NFREQ, 8, 12...  1.01 us
    pallas_call x1, Pallas kernels, local(): pl.pallas_call(last_kernel, out_shape=(whole, whole, shape(1, 2, nx, 16 *...  0.9 us
  transfers between devices with their start and end apart: 3, of which 2 were waited for; matrix products, arithmetic and copies ran while one was open for 0% of the time, Pallas kernels for 6%

profile of v3, /device:TPU:513, one launch (start us, length us, event | category | flops | bytes accessed | tf_op | source)
XLA Modules:
  0.0 42.5 jit_solution(885090792512058578)
XLA Ops:
  0.6 1.8 %shard_map.94 = (f32[3,32,16,128]{3,2,1,0:T(8,128)S(1)}, f32[3,32,16,128]{3,2,1,0:T(8,128)S(1)}, f32[2,32,16,128]{3,2,1,0:T(8,128)S(1)}, f32[14,32,128]{2,1,0:T(...) custom-call(f32[3,32,16,128]{3,2,1,0:T(8,128)} %e_hbm.1, ...), custom_call_target="tpu_custom_call" | custom-call | tf_op jit(solution)/shard_map/pallas_call | solution.py:378
  2.5 3.8 %collective-permute-start = (f32[14,32,128]{2,1,0:T(8,128)S(1)}, f32[14,32,128]{2,1,0:T(8,128)S(1)}, u32[]{:S(2)}, u32[]{:S(2)}) collective-permute-start(f32[14,32,128]{2,1,0:T(8,128)S(1)} %get-tuple-element.23), channel_id=1, source_target_pairs={{1,2},{3,4},{5,6},{7,8},{9,10},{11,12},{13,14},{2,1},{4,3},{6,5},{... | collective-permute-start | bytes 688136 | tf_op jit(solution)/shard_map/ppermute | solution.py:31
  6.2 2.1 %all-gather = f32[28,32,128]{2,1,0:T(8,128)S(1)} all-gather(f32[14,32,128]{2,1,0:T(8,128)S(1)} %get-tuple-element.22), channel_id=2, replica_groups={{0,1},{2,3},{4,5},{6,7},{8,9},{10,11},{12,13},{14,15},{16,17},{18,19},{..., dimensions={0}, use_global_device_ids=true | all-gather | bytes 688128 | tf_op jit(solution)/shard_map/all_gather | solution.py:35
  8.4 1.5 %collective-permute-done.outer_got = f32[14,32,128]{2,1,0:T(8,128)S(1)} collective-permute-done((f32[14,32,128]{2,1,0:T(8,128)S(1)}, f32[14,32,128]{2,1,0:T(8,128)S(1)}, u32[]{:S(2)}, u32[]{:S(2)}) %collective-permute-start) | collective-permute-done | bytes 229408 | tf_op jit(solution)/shard_map/ppermute | solution.py:31
  9.9 0.1 shard_map.95
  10.1 3.1 %collective-permute-start.1 = (f32[14,24,128]{2,1,0:T(8,128)S(1)}, f32[14,24,128]{2,1,0:T(8,128)S(1)}, u32[]{:S(2)}, u32[]{:S(2)}) collective-permute-start(f32[14,24,128]{2,1,0:T(8,128)S(1)} %get-tuple-element.25), channel_id=1, source_target_pairs={{0,16},{32,48},{64,80},{96,112},{128,144},{160,176},{192,208},{224... | collective-permute-start | bytes 516104 | tf_op jit(solution)/shard_map/ppermute | solution.py:31
  13.2 4.9 %collective-permute-start.2 = (f32[14,24,128]{2,1,0:T(8,128)S(1)}, f32[14,24,128]{2,1,0:T(8,128)S(1)}, u32[]{:S(2)}, u32[]{:S(2)}) collective-permute-start(f32[14,24,128]{2,1,0:T(8,128)S(1)} %get-tuple-element.26), channel_id=1, source_target_pairs={{16,32},{48,64},{80,96},{112,128},{144,160},{176,192},{208,224},{2... | collective-permute-start | bytes 516104 | tf_op jit(solution)/shard_map/ppermute | solution.py:31
  18.1 0.1 multiply_cosine_fusion
  18.2 0.1 pad_maximum_fusion.coef_ref
  18.3 2.4 %shard_map.96 = (f32[3,32,16,128]{3,2,1,0:T(8,128)}, f32[3,32,16,128]{3,2,1,0:T(8,128)}, f32[2,8,128]{2,1,0:T(8,128)S(1)}) custom-call(f32[3,32,16,128]{3,2,1,0:T(8,128)S(1)} %get-tuple-element.19.e_ref, f32[3,32,16,128]{3,2,1,0:T(8,128)S(1)} %get-tuple-element.20.h_ref, f32[2,32,16,128]{3,2,1,0:T(8,128)S(1)} %get-tuple-element.21.code_ref, ...), custom_call_target="tpu_custom_call" | custom-call | flops 41943040 | bytes 4194304 | tf_op jit(solution)/shard_map/pallas_call | solution.py:396
  20.7 0.0 collective-permute-done.1.inner_got
  20.7 3.1 %collective-permute-done.2.outer_got = f32[14,24,128]{2,1,0:T(8,128)S(1)} collective-permute-done((f32[14,24,128]{2,1,0:T(8,128)S(1)}, f32[14,24,128]{2,1,0:T(8,128)S(1)}, u32[]{:S(2)}, u32[]{:S(2)}) %collective-permute-start.2) | collective-permute-done | bytes 172064 | tf_op jit(solution)/shard_map/ppermute | solution.py:31
  23.9 1.0 %shard_map.97 = (f32[3,4,16,128]{3,2,1,0:T(8,128)S(1)}, f32[3,4,16,128]{3,2,1,0:T(8,128)S(1)}, f32[16,8,128]{2,1,0:T(8,128)S(1)}) custom-call(f32[3,32,16,128]{3,2,1,0:T(8,128)S(1)} %get-tuple-element.19.e_ref, f32[3,32,16,128]{3,2,1,0:T(8,128)S(1)} %get-tuple-element.20.h_ref, f32[2,32,16,128]{3,2,1,0:T(8,128)S(1)} %get-tuple-element.21.code_ref, ...), custom_call_target="tpu_custom_call" | custom-call | tf_op jit(solution)/shard_map/pallas_call | solution.py:405
  24.9 16.7 %all_to_all.5.got_ref = f32[16,8,128]{2,1,0:T(8,128)S(1)} all-to-all(f32[16,8,128]{2,1,0:T(8,128)S(1)} %get-tuple-element.30), channel_id=1, replica_groups=mesh['gx'=48,'gy'=16] {'gy'}, dimensions={0} | all-to-all | bytes 131072 | tf_op jit(solution)/shard_map/all_to_all | solution.py:414
  41.6 0.9 %shard_map.98 = (f32[3,32,16,128]{3,2,1,0:T(8,128)}, f32[3,32,16,128]{3,2,1,0:T(8,128)}, f32[1,2,32,256]{3,2,1,0:T(8,128)}) custom-call(f32[16,8,128]{2,1,0:T(8,128)S(1)} %all_to_all.5.got_ref, f32[3,4,16,128]{3,2,1,0:T(8,128)S(1)} %get-tuple-element.31.ee_ref, ...), custom_call_target="tpu_custom_call", output_to_operand_aliasing={{0}: (3, {}), {1}: (4, {})} | custom-call | tf_op jit(solution)/shard_map/pallas_call | solution.py:415
  (1 shorter events, 0.0 us)
Async XLA Ops:
  2.5 7.5 %collective-permute-start = (f32[14,32,128]{2,1,0:T(8,128)S(1)}, f32[14,32,128]{2,1,0:T(8,128)S(1)}, u32[]{:S(2)}, u32[]{:S(2)}) collective-permute-start(f32[14,32,128]{2,1,0:T(8,128)S(1)} %get-tuple-element.23), channel_id=1, source_target_pairs={{1,2},{3,4},{5,6},{7,8},{9,10},{11,12},{13,14},{2,1},{4,3},{6,5},{... | collective-permute-start | bytes 688136 | tf_op jit(solution)/shard_map/ppermute | solution.py:31
  10.1 10.7 %collective-permute-start.1 = (f32[14,24,128]{2,1,0:T(8,128)S(1)}, f32[14,24,128]{2,1,0:T(8,128)S(1)}, u32[]{:S(2)}, u32[]{:S(2)}) collective-permute-start(f32[14,24,128]{2,1,0:T(8,128)S(1)} %get-tuple-element.25), channel_id=1, source_target_pairs={{0,16},{32,48},{64,80},{96,112},{128,144},{160,176},{192,208},{224... | collective-permute-start | bytes 516104 | tf_op jit(solution)/shard_map/ppermute | solution.py:31
  13.2 10.7 %collective-permute-start.2 = (f32[14,24,128]{2,1,0:T(8,128)S(1)}, f32[14,24,128]{2,1,0:T(8,128)S(1)}, u32[]{:S(2)}, u32[]{:S(2)}) collective-permute-start(f32[14,24,128]{2,1,0:T(8,128)S(1)} %get-tuple-element.26), channel_id=1, source_target_pairs={{16,32},{48,64},{80,96},{112,128},{144,160},{176,192},{208,224},{2... | collective-permute-start | bytes 516104 | tf_op jit(solution)/shard_map/ppermute | solution.py:31

commit v4 on v3

--- a/solution.py
+++ b/solution.py
@@ -14,8 +14,9 @@
 ALL = tuple(range(8))
 U_MSG = tuple((-1, f) for f in ALL) + tuple((-2, f) for f in (EX, EY, EZ, HX, HZ, FL))
 D_MSG = tuple((0, f) for f in ALL) + tuple((1, f) for f in (EX, EZ))
-R_MSG = tuple((-1, f) for f in ALL) + tuple((-2, f) for f in (EX, EY, EZ, HY, HZ, FL))
-L_MSG = tuple((0, f) for f in ALL) + tuple((1, f) for f in (EY, EZ))
+Q_Y, Q_Z, R_X, R_Y, R_Z, R_FLAG, R_GAIN = range(7)
+P_Y, P_Z, L_GAIN, L_EY, L_EZ = range(5)
+X_MSG = 7
 
 
 MSG = len(U_MSG)
@@ -96,7 +97,7 @@
         pack(outer_ref, inner_ref)
 
 
-def planes_kernel(e_ref, h_ref, code_ref, inner_got, outer_got, inner_ref, outer_ref, third_ref):
+def planes_kernel(e_ref, h_ref, code_ref, inner_got, outer_got, table_ref, inner_ref, outer_ref, third_ref):
     refs = (e_ref, h_ref, code_ref)
     nx = e_ref.shape[1]
     flat = third_ref.reshape(8 * nx * 8, 128)
@@ -117,11 +118,33 @@
     def _():
         fill(inner_got.at[0], outer_got)
 
+    w = Window(table_ref)
+
+    def planes(x):
+        return [jnp.concatenate([field_plane(refs, f, x), third_ref[f, x]], axis=0) for f in ALL]
+
     def pack(right_ref, left_ref):
-        for message, ref, base in ((R_MSG, right_ref, nx), (L_MSG, left_ref, 0)):
-            for i, (at, f) in enumerate(message):
-                ref[i, 0:16] = field_plane(refs, f, base + at)
-                ref[i, 16:24] = third_ref[f, base + at]
+        far, near = planes(nx - 2), planes(nx - 1)
+        _, hy_far, hz_far = w.h_step(far[3:6], far[:3], near[:3], w.h_coefs(far[FL]), False)
+        (ex, ey, ez), (hx, hy, hz) = near[:3], near[3:6]
+        keep, gain = w.h_coefs(near[FL])
+        right_ref[Q_Y] = keep * hy - gain * ((w.next_z(ex) - ex) + ez)
+        right_ref[Q_Z] = keep * hz + gain * (ey + (next_y(ex) - ex))
+        hx = keep * hx - gain * ((next_y(ez) - ez) - (w.next_z(ey) - ey))
+        keep, gain = w.e_coefs(near[FL], near[MT])
+        right_ref[R_X] = keep * ex
+        right_ref[R_Y] = keep * ey + gain * ((hx - w.last_z(hx)) + hz_far)
+        right_ref[R_Z] = keep * ez - gain * (hy_far + (hx - last_y(hx)))
+        right_ref[R_FLAG] = near[FL]
+        right_ref[R_GAIN] = gain
+        near, far = planes(0), planes(1)
+        hx, hy, hz = w.h_step(near[3:6], near[:3], far[:3], w.h_coefs(near[FL]), True)
+        keep, gain = w.e_coefs(near[FL], near[MT])
+        left_ref[P_Y] = keep * near[EY] + gain * ((hx - w.last_z(hx)) - hz)
+        left_ref[P_Z] = keep * near[EZ] + gain * (hy - (hx - last_y(hx)))
+        left_ref[L_GAIN] = gain
+        left_ref[L_EY] = near[EY]
+        left_ref[L_EZ] = near[EZ]
 
     second_x = is_second("gx")
 
@@ -192,11 +215,18 @@
         ez = keep * e[2][:rows] + gain * ((hy - h_last[1][:rows]) - (hx - hx_y))
         return ex, ey, ez
 
-    def run(self, planes, first, last, keep_first_step, store, skew):
+    def run(self, planes, first, last, keep_first_step, store, skew, behind=None, ahead=None):
         e0, h0, hc, ec, h1, e1, h2 = {}, {}, {}, {}, {}, {}, {}
+        begin = first - 2 if behind is None else first - 1
 
         def fetch(x):
-            if x not in e0:
+            if x in e0:
+                return
+            if ahead is not None and x == last:
+                e0[x] = (None, ahead[L_EY], ahead[L_EZ])
+            elif behind is not None and x < first:
+                e0[x], hc[x] = None, self.h_coefs(behind[R_FLAG])
+            else:
                 p = planes(x)
                 e0[x], h0[x] = p[:3], p[3:6]
                 if x <= last:
@@ -206,18 +236,30 @@
 
         for turn in range(first - 2, last + 2 + 3 * skew):
             x = turn
-            if x <= last:
+            if begin <= x <= last - (ahead is not None):
                 fetch(x)
                 fetch(x + 1)
-                h1[x] = self.h_step(h0[x], e0[x], e0[x + 1], hc[x], x > first - 2)
+                if e0[x] is None:
+                    gain = hc[x][1]
+                    h1[x] = (None, behind[Q_Y] + gain * e0[x + 1][2], behind[Q_Z] - gain * e0[x + 1][1])
+                else:
+                    h1[x] = self.h_step(h0[x], e0[x], e0[x + 1], hc[x], x > begin or behind is not None)
             x = turn - skew
-            if first - 1 <= x <= last:
+            if behind is not None and x == first - 1:
+                _, hy, hz = h1[x]
+                gain = behind[R_GAIN]
+                ex = behind[R_X] + gain * ((hz - last_y(hz)) - (hy - self.last_z(hy)))
+                e1[x] = (ex, behind[R_Y] - gain * hz, behind[R_Z] + gain * hy)
+            elif ahead is not None and x == last:
+                _, hy, hz = h1[x - 1]
+                e1[x] = (None, ahead[P_Y] + ahead[L_GAIN] * hz, ahead[P_Z] - ahead[L_GAIN] * hy)
+            elif first - 1 <= x <= last:
                 e1[x] = self.e_step(e0[x], h1[x], h1[x - 1], ec[x])
                 if first <= x < last:
                     keep_first_step(x, e1[x])
             x = turn - 2 * skew - 1
             if first - 1 <= x < last:
-                h2[x] = self.h_step(h1[x], e1[x], e1[x + 1], hc[x], True)
+                h2[x] = self.h_step(h1[x], e1[x], e1[x + 1], hc[x], x >= first)
             x = turn - 3 * skew - 1
             if first <= x < last:
                 store(x, self.e_step(e1[x], h2[x], h2[x - 1], ec[x], 16), h2[x])
@@ -275,7 +317,7 @@
         copy.wait()
 
 
-def edge_kernel(e_ref, h_ref, code_ref, third_ref, inner_got, outer_got, table_ref, tile_ref, coef_ref,
+def edge_kernel(e_ref, h_ref, code_ref, third_ref, outer_got, inner_got, table_ref, tile_ref, coef_ref,
                 eo_ref, ho_ref, part_ref, first_ref, right_ref, left_ref):
     refs = (e_ref, h_ref, code_ref)
     nx = e_ref.shape[1]
@@ -292,10 +334,7 @@
         left_ref[...] = outer_got[...]
 
     def planes(x):
-        if 0 <= x < nx:
-            return [jnp.concatenate([field_plane(refs, f, x), third_ref[f, x]], axis=0) for f in ALL]
-        message, ref, at = (R_MSG, right_ref, x) if x < 0 else (L_MSG, left_ref, x - nx)
-        return [ref[message.index((at, f))] if (at, f) in message else None for f in ALL]
+        return [jnp.concatenate([field_plane(refs, f, x), third_ref[f, x]], axis=0) for f in ALL]
 
     def slot(x):
         return x if x < 2 else x - nx + 4
@@ -310,7 +349,9 @@
             ho_ref[c, slot(x)] = h[c][0:16]
 
     window = Window(table_ref)
-    for _ in zip(*(window.run(planes, at, at + 2, keep_first_step, store, EDGE_SKEW) for at in (0, nx - 2))):
+    low = window.run(planes, 0, 2, keep_first_step, store, EDGE_SKEW, behind=right_ref)
+    high = window.run(planes, nx - 2, nx, keep_first_step, store, EDGE_SKEW, ahead=left_ref)
+    for _ in zip(low, high):
         pass
     tiles = []
     for step, ref in enumerate((first_ref, eo_ref)):
@@ -389,9 +430,9 @@
     outer, inner = swapped(outer, "gy", 1), gather_inner(inner, "gy")
     inner, outer, third = pl.pallas_call(
         planes_kernel,
-        out_shape=(shape(MSG, 24, nz), shape(MSG, 24, nz), shape(8, nx, 8, nz)),
-        in_specs=[VM] * 5, out_specs=(VM,) * 3, compiler_params=LIMIT,
-    )(e, h, code, inner, outer)
+        out_shape=(shape(X_MSG, 24, nz), shape(X_MSG, 24, nz), shape(8, nx, 8, nz)),
+        in_specs=[VM] * 6, out_specs=(VM,) * 3, compiler_params=LIMIT,
+    )(e, h, code, inner, outer, table)
     outer, inner = swapped(outer, "gx", 1), swapped(inner, "gx", 0)
     ei, hi, tile = pl.pallas_call(
         inner_kernel,
@@ -408,9 +449,9 @@
         in_specs=[VM] * 8 + [SM], out_specs=(VM,) * 3,
         scratch_shapes=[
             pltpu.VMEM((2, 4, ny, nz), jnp.float32),
-            pltpu.VMEM((MSG, 24, nz), jnp.float32), pltpu.VMEM((MSG, 24, nz), jnp.float32),
+            pltpu.VMEM((X_MSG, 24, nz), jnp.float32), pltpu.VMEM((X_MSG, 24, nz), jnp.float32),
         ], compiler_params=LIMIT,
-    )(e, h, code, third, inner, outer, table, tile, coef)
+    )(e, h, code, third, outer, inner, table, tile, coef)
     got = lax.all_to_all(part, "gy", split_axis=0, concat_axis=0, tiled=True)
     electric_out, magnetic_out, spectra = pl.pallas_call(
         last_kernel,

time: 42.7 us -> 41.1 us (0.963)
  waiting for transfers between devices: 4.65 us -> 2.62 us
  blocking collectives: 18.9 us -> 19.7 us
  starting transfers between devices: 11.8 us -> 11.3 us
    ppermute x3, waiting for transfers between devices: 4.65 us -> 2.62 us  [swapped(): return lax.ppermute(x, axis, pairs + [(b, a) for a, b in pairs])]
    all_to_all x1, blocking collectives: 16.7 us -> 17.5 us  [local(): got = lax.all_to_all(part, 'gy', split_axis=0, concat_axis=0, tiled=True)]
    ppermute x3, starting transfers between devices: 11.8 us -> 11.3 us  [swapped(): return lax.ppermute(x, axis, pairs + [(b, a) for a, b in pairs])]
where the time goes in v4:
time: 41.1 us; the launch traced here: 40.9 us
  blocking collectives  19.7 us (48%)
  starting transfers between devices  11.3 us (27%)
  Pallas kernels  6.43 us (16%)
  waiting for transfers between devices  2.62 us (6%)
  between operations  0.7 us (2%)
    all_to_all x1, blocking collectives, local(): got = lax.all_to_all(part, 'gy', split_axis=0, concat_axis=0, tiled=True)  17.5 us
    ppermute x3, starting transfers between devices, swapped(): return lax.ppermute(x, axis, pairs + [(b, a) for a, b in pairs])  11.3 us
    ppermute x3, waiting for transfers between devices, swapped(): return lax.ppermute(x, axis, pairs + [(b, a) for a, b in pairs])  2.62 us
    pallas_call x1, Pallas kernels, local(): pl.pallas_call(inner_kernel, out_shape=(whole, whole, shape(2, 8, 128)),...  2.42 us
    all_gather x1, blocking collectives, gather_inner(): lax.all_gather(x, axis, axis=0, axis_index_groups=[list(p) for p in paire...  2.14 us
    pallas_call x1, Pallas kernels, local(): pl.pallas_call(load_kernel, out_shape=(whole, whole, shape(2, nx, ny, nz)...  1.82 us
    pallas_call x1, Pallas kernels, local(): pl.pallas_call(edge_kernel, out_shape=(edge, edge, shape(2 * NFREQ, 8, 12...  1.02 us
    pallas_call x1, Pallas kernels, local(): pl.pallas_call(last_kernel, out_shape=(whole, whole, shape(1, 2, nx, 16 *...  0.9 us
  transfers between devices with their start and end apart: 3, of which 2 were waited for; matrix products, arithmetic and copies ran while one was open for 0% of the time, Pallas kernels for 6%

profile of v4, /device:TPU:513, one launch (start us, length us, event | category | flops | bytes accessed | tf_op | source)
XLA Modules:
  0.0 40.9 jit_solution(357718615471462926)
XLA Ops:
  0.6 1.8 %shard_map.94 = (f32[3,32,16,128]{3,2,1,0:T(8,128)S(1)}, f32[3,32,16,128]{3,2,1,0:T(8,128)S(1)}, f32[2,32,16,128]{3,2,1,0:T(8,128)S(1)}, f32[14,32,128]{2,1,0:T(...) custom-call(f32[3,32,16,128]{3,2,1,0:T(8,128)} %e_hbm.1, ...), custom_call_target="tpu_custom_call" | custom-call | tf_op jit(solution)/shard_map/pallas_call | solution.py:419
  2.5 3.8 %collective-permute-start = (f32[14,32,128]{2,1,0:T(8,128)S(1)}, f32[14,32,128]{2,1,0:T(8,128)S(1)}, u32[]{:S(2)}, u32[]{:S(2)}) collective-permute-start(f32[14,32,128]{2,1,0:T(8,128)S(1)} %get-tuple-element.23), channel_id=1, source_target_pairs={{1,2},{3,4},{5,6},{7,8},{9,10},{11,12},{13,14},{2,1},{4,3},{6,5},{... | collective-permute-start | bytes 688136 | tf_op jit(solution)/shard_map/ppermute | solution.py:32
  6.2 2.1 %all-gather = f32[28,32,128]{2,1,0:T(8,128)S(1)} all-gather(f32[14,32,128]{2,1,0:T(8,128)S(1)} %get-tuple-element.22), channel_id=2, replica_groups={{0,1},{2,3},{4,5},{6,7},{8,9},{10,11},{12,13},{14,15},{16,17},{18,19},{..., dimensions={0}, use_global_device_ids=true | all-gather | bytes 688128 | tf_op jit(solution)/shard_map/all_gather | solution.py:36
  8.4 0.1 multiply_cosine_fusion
  8.5 1.4 %collective-permute-done.outer_got = f32[14,32,128]{2,1,0:T(8,128)S(1)} collective-permute-done((f32[14,32,128]{2,1,0:T(8,128)S(1)}, f32[14,32,128]{2,1,0:T(8,128)S(1)}, u32[]{:S(2)}, u32[]{:S(2)}) %collective-permute-start) | collective-permute-done | bytes 229408 | tf_op jit(solution)/shard_map/ppermute | solution.py:32
  9.9 0.3 shard_map.95
  10.2 5.6 %collective-permute-start.1 = (f32[7,24,128]{2,1,0:T(8,128)S(1)}, f32[7,24,128]{2,1,0:T(8,128)S(1)}, u32[]{:S(2)}, u32[]{:S(2)}) collective-permute-start(f32[7,24,128]{2,1,0:T(8,128)S(1)} %get-tuple-element.26), channel_id=1, source_target_pairs={{16,32},{48,64},{80,96},{112,128},{144,160},{176,192},{208,224},{2... | collective-permute-start | bytes 258056 | tf_op jit(solution)/shard_map/ppermute | solution.py:32
  15.8 1.9 %collective-permute-start.2 = (f32[7,24,128]{2,1,0:T(8,128)S(1)}, f32[7,24,128]{2,1,0:T(8,128)S(1)}, u32[]{:S(2)}, u32[]{:S(2)}) collective-permute-start(f32[7,24,128]{2,1,0:T(8,128)S(1)} %get-tuple-element.27), channel_id=1, source_target_pairs={{0,16},{32,48},{64,80},{96,112},{128,144},{160,176},{192,208},{224... | collective-permute-start | bytes 258056 | tf_op jit(solution)/shard_map/ppermute | solution.py:32
  17.7 0.1 pad_maximum_fusion.coef_ref
  17.8 2.4 %shard_map.96 = (f32[3,32,16,128]{3,2,1,0:T(8,128)}, f32[3,32,16,128]{3,2,1,0:T(8,128)}, f32[2,8,128]{2,1,0:T(8,128)S(1)}) custom-call(f32[3,32,16,128]{3,2,1,0:T(8,128)S(1)} %get-tuple-element.19.e_ref, f32[3,32,16,128]{3,2,1,0:T(8,128)S(1)} %get-tuple-element.20.h_ref, f32[2,32,16,128]{3,2,1,0:T(8,128)S(1)} %get-tuple-element.21.code_ref, ...), custom_call_target="tpu_custom_call" | custom-call | flops 41943040 | bytes 4194304 | tf_op jit(solution)/shard_map/pallas_call | solution.py:437
  20.2 0.0 collective-permute-done.1.outer_got
  20.2 1.2 %collective-permute-done.2.inner_got = f32[7,24,128]{2,1,0:T(8,128)S(1)} collective-permute-done((f32[7,24,128]{2,1,0:T(8,128)S(1)}, f32[7,24,128]{2,1,0:T(8,128)S(1)}, u32[]{:S(2)}, u32[]{:S(2)}) %collective-permute-start.2) | collective-permute-done | bytes 86048 | tf_op jit(solution)/shard_map/ppermute | solution.py:32
  21.4 1.0 %shard_map.97 = (f32[3,4,16,128]{3,2,1,0:T(8,128)S(1)}, f32[3,4,16,128]{3,2,1,0:T(8,128)S(1)}, f32[16,8,128]{2,1,0:T(8,128)S(1)}) custom-call(f32[3,32,16,128]{3,2,1,0:T(8,128)S(1)} %get-tuple-element.19.e_ref, f32[3,32,16,128]{3,2,1,0:T(8,128)S(1)} %get-tuple-element.20.h_ref, f32[2,32,16,128]{3,2,1,0:T(8,128)S(1)} %get-tuple-element.21.code_ref, ...), custom_call_target="tpu_custom_call" | custom-call | tf_op jit(solution)/shard_map/pallas_call | solution.py:446
  22.5 17.5 %all_to_all.5.got_ref = f32[16,8,128]{2,1,0:T(8,128)S(1)} all-to-all(f32[16,8,128]{2,1,0:T(8,128)S(1)} %get-tuple-element.30), channel_id=1, replica_groups=mesh['gx'=48,'gy'=16] {'gy'}, dimensions={0} | all-to-all | bytes 131072 | tf_op jit(solution)/shard_map/all_to_all | solution.py:455
  40.0 0.9 %shard_map.98 = (f32[3,32,16,128]{3,2,1,0:T(8,128)}, f32[3,32,16,128]{3,2,1,0:T(8,128)}, f32[1,2,32,256]{3,2,1,0:T(8,128)}) custom-call(f32[16,8,128]{2,1,0:T(8,128)S(1)} %all_to_all.5.got_ref, f32[3,4,16,128]{3,2,1,0:T(8,128)S(1)} %get-tuple-element.31.ee_ref, ...), custom_call_target="tpu_custom_call", output_to_operand_aliasing={{0}: (3, {}), {1}: (4, {})} | custom-call | tf_op jit(solution)/shard_map/pallas_call | solution.py:456
  (1 shorter events, 0.0 us)
Async XLA Ops:
  2.5 7.5 %collective-permute-start = (f32[14,32,128]{2,1,0:T(8,128)S(1)}, f32[14,32,128]{2,1,0:T(8,128)S(1)}, u32[]{:S(2)}, u32[]{:S(2)}) collective-permute-start(f32[14,32,128]{2,1,0:T(8,128)S(1)} %get-tuple-element.23), channel_id=1, source_target_pairs={{1,2},{3,4},{5,6},{7,8},{9,10},{11,12},{13,14},{2,1},{4,3},{6,5},{... | collective-permute-start | bytes 688136 | tf_op jit(solution)/shard_map/ppermute | solution.py:32
  10.2 10.0 %collective-permute-start.1 = (f32[7,24,128]{2,1,0:T(8,128)S(1)}, f32[7,24,128]{2,1,0:T(8,128)S(1)}, u32[]{:S(2)}, u32[]{:S(2)}) collective-permute-start(f32[7,24,128]{2,1,0:T(8,128)S(1)} %get-tuple-element.26), channel_id=1, source_target_pairs={{16,32},{48,64},{80,96},{112,128},{144,160},{176,192},{208,224},{2... | collective-permute-start | bytes 258056 | tf_op jit(solution)/shard_map/ppermute | solution.py:32
  15.8 5.6 %collective-permute-start.2 = (f32[7,24,128]{2,1,0:T(8,128)S(1)}, f32[7,24,128]{2,1,0:T(8,128)S(1)}, u32[]{:S(2)}, u32[]{:S(2)}) collective-permute-start(f32[7,24,128]{2,1,0:T(8,128)S(1)} %get-tuple-element.27), channel_id=1, source_target_pairs={{0,16},{32,48},{64,80},{96,112},{128,144},{160,176},{192,208},{224... | collective-permute-start | bytes 258056 | tf_op jit(solution)/shard_map/ppermute | solution.py:32

commit v5 on v4

--- a/solution.py
+++ b/solution.py
@@ -41,30 +41,51 @@
 
 
 def field_plane(refs, f, x):
-    e_ref, h_ref, code_ref = refs
+    e_ref, h_ref, m_ref, p_ref = refs
     if f < 3:
         return e_ref[f, x]
     if f < 6:
         return h_ref[f - 3, x]
-    return code_ref[f - FL, x]
-
-
-def field_rows(refs, f, y):
-    e_ref, h_ref, code_ref = refs
-    ref, at = (e_ref, f) if f < 3 else (h_ref, f - 3) if f < 6 else (code_ref, f - FL)
-    count, nx, ny = ref.shape[0], ref.shape[1], ref.shape[2]
-    return ref.reshape(count * nx * ny, 128)[pl.ds(at * nx * ny + y, nx, stride=ny)]
-
-
-def load_kernel(e_hbm, h_hbm, m_hbm, p_hbm, eps_hbm, sigma_hbm, omega_hbm,
-                e_ref, h_ref, code_ref, inner_ref, outer_ref, table_ref, omega_ref, m_ref, p_ref, sigma_ref, eps_ref, sems):
-    pairs = [(e_hbm.at[c], e_ref.at[c]) for c in range(3)] + [(h_hbm.at[c], h_ref.at[c]) for c in range(3)]
-    pairs += [(m_hbm, m_ref), (p_hbm, p_ref), (eps_hbm, eps_ref), (sigma_hbm, sigma_ref), (omega_hbm, omega_ref)]
-    copies = [pltpu.make_async_copy(src, dst, sems.at[i]) for i, (src, dst) in enumerate(pairs)]
-    for copy in copies:
-        copy.start()
-    for copy in copies:
-        copy.wait()
+    source = p_ref if f == FL else m_ref
+    return source[x].astype(jnp.float32) + 1.0
+
+
+def rows_kernel(e_hbm, h_hbm, m_hbm, p_hbm, eps_hbm, sigma_hbm, omega_hbm,
+                inner_ref, outer_ref, table_ref, omega_ref, up_codes, down_codes, sigma_ref, eps_ref, sems):
+    ny = m_hbm.shape[1]
+
+    def fetch(up_ref, down_ref):
+        pairs = []
+        for ref, last in ((up_ref, ny - 1), (down_ref, 0)):
+            pairs += [(e_hbm.at[:, :, last, :], ref.at[0:3]), (h_hbm.at[:, :, last, :], ref.at[3:6])]
+        pairs += [
+            (p_hbm.at[:, ny - 1, :], up_codes.at[0]), (m_hbm.at[:, ny - 1, :], up_codes.at[1]),
+            (p_hbm.at[:, ny - 2, :], up_codes.at[2]),
+            (p_hbm.at[:, 0, :], down_codes.at[0]), (m_hbm.at[:, 0, :], down_codes.at[1]),
+            (e_hbm.at[:, :, ny - 2, :], up_ref.at[8:11]),
+            (h_hbm.at[0, :, ny - 2, :], up_ref.at[11]), (h_hbm.at[2, :, ny - 2, :], up_ref.at[12]),
+            (e_hbm.at[0, :, 1, :], down_ref.at[8]), (e_hbm.at[2, :, 1, :], down_ref.at[9]),
+            (eps_hbm, eps_ref), (sigma_hbm, sigma_ref), (omega_hbm, omega_ref),
+        ]
+        copies = [pltpu.make_async_copy(src, dst, sems.at[i]) for i, (src, dst) in enumerate(pairs)]
+        for copy in copies:
+            copy.start()
+        for copy in copies:
+            copy.wait()
+        up_ref[6:8] = up_codes[0:2].astype(jnp.float32) + 1.0
+        up_ref[13] = up_codes[2].astype(jnp.float32) + 1.0
+        down_ref[6:8] = down_codes[...].astype(jnp.float32) + 1.0
+
+    second = is_second("gy")
+
+    @pl.when(second == 0)
+    def _():
+        fetch(inner_ref, outer_ref)
+
+    @pl.when(second == 1)
+    def _():
+        fetch(outer_ref, inner_ref)
+
     sigma = sigma_ref[...]
     s_mag = sigma * time_step / 2.0
     table_ref[0:1] = (1.0 - s_mag) / (1.0 + s_mag)
@@ -75,30 +96,10 @@
         table_ref[2 + k:3 + k] = (1.0 - s_ele) / (1.0 + s_ele)
         table_ref[6 + k:7 + k] = time_step / (eps * (1.0 + s_ele))
         table_ref[10 + k:11 + k] = time_step / eps
-    code_ref[0] = p_ref[...].astype(jnp.float32) + 1.0
-    code_ref[1] = m_ref[...].astype(jnp.float32) + 1.0
-    refs = (e_ref, h_ref, code_ref)
-    ny = m_ref.shape[1]
-
-    def pack(up_ref, down_ref):
-        for i, (at, f) in enumerate(U_MSG):
-            up_ref[i] = field_rows(refs, f, ny + at)
-        for i, (at, f) in enumerate(D_MSG):
-            down_ref[i] = field_rows(refs, f, at)
-
-    second = is_second("gy")
-
-    @pl.when(second == 0)
-    def _():
-        pack(inner_ref, outer_ref)
-
-    @pl.when(second == 1)
-    def _():
-        pack(outer_ref, inner_ref)
-
-
-def planes_kernel(e_ref, h_ref, code_ref, inner_got, outer_got, table_ref, inner_ref, outer_ref, third_ref):
-    refs = (e_ref, h_ref, code_ref)
+
+
+def planes_kernel(e_ref, h_ref, m_ref, p_ref, inner_got, outer_got, table_ref, inner_ref, outer_ref, third_ref):
+    refs = (e_ref, h_ref, m_ref, p_ref)
     nx = e_ref.shape[1]
     flat = third_ref.reshape(8 * nx * 8, 128)
 
@@ -285,8 +286,8 @@
     return out
 
 
-def inner_kernel(e_ref, h_ref, code_ref, third_ref, table_ref, eo_hbm, ho_hbm, tile_ref, first_ref, eo_ref, ho_ref, sems):
-    refs = (e_ref, h_ref, code_ref)
+def inner_kernel(e_ref, h_ref, m_ref, p_ref, third_ref, table_ref, eo_hbm, ho_hbm, tile_ref, first_ref, eo_ref, ho_ref, sems):
+    refs = (e_ref, h_ref, m_ref, p_ref)
     nx = e_ref.shape[1]
 
     def planes(x):
@@ -317,9 +318,9 @@
         copy.wait()
 
 
-def edge_kernel(e_ref, h_ref, code_ref, third_ref, outer_got, inner_got, table_ref, tile_ref, coef_ref,
+def edge_kernel(e_ref, h_ref, m_ref, p_ref, third_ref, outer_got, inner_got, table_ref, tile_ref, coef_ref,
                 eo_ref, ho_ref, part_ref, first_ref, right_ref, left_ref):
-    refs = (e_ref, h_ref, code_ref)
+    refs = (e_ref, h_ref, m_ref, p_ref)
     nx = e_ref.shape[1]
     second = is_second("gx")
 
@@ -416,42 +417,42 @@
     moments = jnp.arange(1, STEPS + 1, dtype=jnp.float32)[:, None] * time_step
     whole, edge = shape(3, nx, ny, nz), shape(3, 4, ny, nz)
 
-    e, h, code, inner, outer, table, omega = pl.pallas_call(
-        load_kernel,
-        out_shape=(whole, whole, shape(2, nx, ny, nz), shape(MSG, nx, nz), shape(MSG, nx, nz), shape(16, nz), shape(1, NFREQ)),
-        in_specs=[HBM] * 7, out_specs=(VM,) * 7,
+    fields = (electric, magnetic, material, pml_flags)
+    inner, outer, table, omega = pl.pallas_call(
+        rows_kernel,
+        out_shape=(shape(MSG, nx, nz), shape(MSG, nx, nz), shape(16, nz), shape(1, NFREQ)),
+        in_specs=[HBM] * 7, out_specs=(VM,) * 4,
         scratch_shapes=[
-            pltpu.VMEM((nx, ny, nz), jnp.int32), pltpu.VMEM((nx, ny, nz), jnp.int32),
-            pltpu.VMEM((1, nz), jnp.float32), pltpu.SMEM((NMAT,), jnp.float32), pltpu.SemaphoreType.DMA((11,)),
+            pltpu.VMEM((3, nx, nz), jnp.int32), pltpu.VMEM((2, nx, nz), jnp.int32),
+            pltpu.VMEM((1, nz), jnp.float32), pltpu.SMEM((NMAT,), jnp.float32), pltpu.SemaphoreType.DMA((17,)),
         ], compiler_params=LIMIT,
-    )(*(pltpu.with_memory_space_constraint(a, pltpu.HBM) for a in (
-        electric, magnetic, material, pml_flags, permittivity, pml_sigma[None], omega[None])))
+    )(*(pltpu.with_memory_space_constraint(a, pltpu.HBM) for a in (*fields, permittivity, pml_sigma[None], omega[None])))
     coef = jnp.concatenate([jnp.cos(omega * moments), -jnp.sin(omega * moments)], axis=1)
     outer, inner = swapped(outer, "gy", 1), gather_inner(inner, "gy")
     inner, outer, third = pl.pallas_call(
         planes_kernel,
         out_shape=(shape(X_MSG, 24, nz), shape(X_MSG, 24, nz), shape(8, nx, 8, nz)),
-        in_specs=[VM] * 6, out_specs=(VM,) * 3, compiler_params=LIMIT,
-    )(e, h, code, inner, outer, table)
+        in_specs=[VM] * 7, out_specs=(VM,) * 3, compiler_params=LIMIT,
+    )(*fields, inner, outer, table)
     outer, inner = swapped(outer, "gx", 1), swapped(inner, "gx", 0)
     ei, hi, tile = pl.pallas_call(
         inner_kernel,
         out_shape=(whole, whole, shape(2, 8, 128)),
-        in_specs=[VM] * 5, out_specs=(HBM, HBM, VM),
+        in_specs=[VM] * 6, out_specs=(HBM, HBM, VM),
         scratch_shapes=[
             pltpu.VMEM((2, nx, ny, nz), jnp.float32), pltpu.VMEM((3, nx, ny, nz), jnp.float32),
             pltpu.VMEM((3, nx, ny, nz), jnp.float32), pltpu.SemaphoreType.DMA((2 * len(CUTS),)),
         ], compiler_params=LIMIT, cost_estimate=cost(40 << 20),
-    )(e, h, code, third, table)
+    )(*fields, third, table)
     ee, he, part = pl.pallas_call(
         edge_kernel,
         out_shape=(edge, edge, shape(2 * NFREQ, 8, 128)),
-        in_specs=[VM] * 8 + [SM], out_specs=(VM,) * 3,
+        in_specs=[VM] * 9 + [SM], out_specs=(VM,) * 3,
         scratch_shapes=[
             pltpu.VMEM((2, 4, ny, nz), jnp.float32),
             pltpu.VMEM((X_MSG, 24, nz), jnp.float32), pltpu.VMEM((X_MSG, 24, nz), jnp.float32),
         ], compiler_params=LIMIT,
-    )(e, h, code, third, outer, inner, table, tile, coef)
+    )(*fields, third, outer, inner, table, tile, coef)
     got = lax.all_to_all(part, "gy", split_axis=0, concat_axis=0, tiled=True)
     electric_out, magnetic_out, spectra = pl.pallas_call(
         last_kernel,

time: 41.1 us -> 40.6 us (0.988)
  Pallas kernels: 6.43 us -> 5.92 us
    pallas_call x1, Pallas kernels: 1.82 us -> 1.3 us  [local(): pl.pallas_call(rows_kernel, out_shape=(shape(MSG, nx, nz), shape(MSG, nx,...]
where the time goes in v5:
time: 40.6 us; the launch traced here: 40.4 us
  blocking collectives  19.6 us (48%)
  starting transfers between devices  11.3 us (28%)
  Pallas kernels  5.92 us (15%)
  waiting for transfers between devices  2.62 us (6%)
  between operations  0.74 us (2%)
    all_to_all x1, blocking collectives, local(): got = lax.all_to_all(part, 'gy', split_axis=0, concat_axis=0, tiled=True)  17.4 us
    ppermute x3, starting transfers between devices, swapped(): return lax.ppermute(x, axis, pairs + [(b, a) for a, b in pairs])  11.3 us
    ppermute x3, waiting for transfers between devices, swapped(): return lax.ppermute(x, axis, pairs + [(b, a) for a, b in pairs])  2.62 us
    pallas_call x1, Pallas kernels, local(): pl.pallas_call(inner_kernel, out_shape=(whole, whole, shape(2, 8, 128)),...  2.41 us
    all_gather x1, blocking collectives, gather_inner(): lax.all_gather(x, axis, axis=0, axis_index_groups=[list(p) for p in paire...  2.27 us
    pallas_call x1, Pallas kernels, local(): pl.pallas_call(rows_kernel, out_shape=(shape(MSG, nx, nz), shape(MSG, nx,...  1.3 us
    pallas_call x1, Pallas kernels, local(): pl.pallas_call(edge_kernel, out_shape=(edge, edge, shape(2 * NFREQ, 8, 12...  1.02 us
    pallas_call x1, Pallas kernels, local(): pl.pallas_call(last_kernel, out_shape=(whole, whole, shape(1, 2, nx, 16 *...  0.9 us
  transfers between devices with their start and end apart: 3, of which 2 were waited for; matrix products, arithmetic and copies ran while one was open for 0% of the time, Pallas kernels for 6%

profile of v5, /device:TPU:513, one launch (start us, length us, event | category | flops | bytes accessed | tf_op | source)
XLA Modules:
  0.0 40.4 jit_solution(2610471872334552426)
XLA Ops:
  0.6 0.0 copy-start
  0.6 0.0 copy-start.1
  0.7 1.3 %shard_map.94 = (f32[14,32,128]{2,1,0:T(8,128)S(1)}, f32[14,32,128]{2,1,0:T(8,128)S(1)}, f32[16,128]{1,0:T(8,128)S(1)}, f32[1,8]{1,0:T(1,128)S(1)}) custom-call(f32[3,32,16,128]{3,2,1,0:T(8,128)} %e_ref.5, f32[3,32,16,128]{3,2,1,0:T(8,128)} %h_ref.5, s32[32,16,128]{2,1,0:T(8,128)} %m_ref.5, s32[32,16,128]{2,1,0:T(8,128)} %p_ref.5, f32[4]{0:T(128)} %eps_hbm.1, ...), custom_call_target="tpu_custom_call" | custom-call | tf_op jit(solution)/shard_map/pallas_call | solution.py:421
  2.0 3.8 %collective-permute-start = (f32[14,32,128]{2,1,0:T(8,128)S(1)}, f32[14,32,128]{2,1,0:T(8,128)S(1)}, u32[]{:S(2)}, u32[]{:S(2)}) collective-permute-start(f32[14,32,128]{2,1,0:T(8,128)S(1)} %get-tuple-element.17), channel_id=1, source_target_pairs={{1,2},{3,4},{5,6},{7,8},{9,10},{11,12},{13,14},{2,1},{4,3},{6,5},{... | collective-permute-start | bytes 688136 | tf_op jit(solution)/shard_map/ppermute | solution.py:32
  5.7 0.0 copy-start.2
  5.7 0.0 copy-start.3
  5.8 2.3 %all-gather = f32[28,32,128]{2,1,0:T(8,128)S(1)} all-gather(f32[14,32,128]{2,1,0:T(8,128)S(1)} %get-tuple-element.16), channel_id=2, replica_groups={{0,1},{2,3},{4,5},{6,7},{8,9},{10,11},{12,13},{14,15},{16,17},{18,19},{..., dimensions={0}, use_global_device_ids=true | all-gather | bytes 688128 | tf_op jit(solution)/shard_map/all_gather | solution.py:36
  8.0 0.1 multiply_cosine_fusion
  8.1 1.3 %collective-permute-done.outer_got = f32[14,32,128]{2,1,0:T(8,128)S(1)} collective-permute-done((f32[14,32,128]{2,1,0:T(8,128)S(1)}, f32[14,32,128]{2,1,0:T(8,128)S(1)}, u32[]{:S(2)}, u32[]{:S(2)}) %collective-permute-start) | collective-permute-done | bytes 229408 | tf_op jit(solution)/shard_map/ppermute | solution.py:32
  9.4 0.0 copy-done
  9.4 0.0 copy-done.1
  9.4 0.0 copy-done.2
  9.4 0.0 copy-done.3
  9.4 0.3 shard_map.95
  9.7 5.6 %collective-permute-start.1 = (f32[7,24,128]{2,1,0:T(8,128)S(1)}, f32[7,24,128]{2,1,0:T(8,128)S(1)}, u32[]{:S(2)}, u32[]{:S(2)}) collective-permute-start(f32[7,24,128]{2,1,0:T(8,128)S(1)} %get-tuple-element.20), channel_id=1, source_target_pairs={{16,32},{48,64},{80,96},{112,128},{144,160},{176,192},{208,224},{2... | collective-permute-start | bytes 258056 | tf_op jit(solution)/shard_map/ppermute | solution.py:32
  15.3 1.9 %collective-permute-start.2 = (f32[7,24,128]{2,1,0:T(8,128)S(1)}, f32[7,24,128]{2,1,0:T(8,128)S(1)}, u32[]{:S(2)}, u32[]{:S(2)}) collective-permute-start(f32[7,24,128]{2,1,0:T(8,128)S(1)} %get-tuple-element.21), channel_id=1, source_target_pairs={{0,16},{32,48},{64,80},{96,112},{128,144},{160,176},{192,208},{224... | collective-permute-start | bytes 258056 | tf_op jit(solution)/shard_map/ppermute | solution.py:32
  17.3 0.1 pad_maximum_fusion.coef_ref
  17.3 2.4 %shard_map.96 = (f32[3,32,16,128]{3,2,1,0:T(8,128)}, f32[3,32,16,128]{3,2,1,0:T(8,128)}, f32[2,8,128]{2,1,0:T(8,128)S(1)}) custom-call(f32[3,32,16,128]{3,2,1,0:T(8,128)S(1)} %copy-done, f32[3,32,16,128]{3,2,1,0:T(8,128)S(1)} %copy-done.1, s32[32,16,128]{2,1,0:T(8,128)S(1)} %copy-done.2, s32[32,16,128]{2,1,0:T(8,128)S(1)} %copy-done.3, ...), custom_call_target="tpu_custom_call" | custom-call | flops 41943040 | bytes 4194304 | tf_op jit(solution)/shard_map/pallas_call | solution.py:438
  19.8 0.0 collective-permute-done.1.outer_got
  19.8 1.3 %collective-permute-done.2.inner_got = f32[7,24,128]{2,1,0:T(8,128)S(1)} collective-permute-done((f32[7,24,128]{2,1,0:T(8,128)S(1)}, f32[7,24,128]{2,1,0:T(8,128)S(1)}, u32[]{:S(2)}, u32[]{:S(2)}) %collective-permute-start.2) | collective-permute-done | bytes 86048 | tf_op jit(solution)/shard_map/ppermute | solution.py:32
  21.1 1.0 %shard_map.97 = (f32[3,4,16,128]{3,2,1,0:T(8,128)S(1)}, f32[3,4,16,128]{3,2,1,0:T(8,128)S(1)}, f32[16,8,128]{2,1,0:T(8,128)S(1)}) custom-call(f32[3,32,16,128]{3,2,1,0:T(8,128)S(1)} %copy-done, f32[3,32,16,128]{3,2,1,0:T(8,128)S(1)} %copy-done.1, s32[32,16,128]{2,1,0:T(8,128)S(1)} %copy-done.2, s32[32,16,128]{2,1,0:T(8,128)S(1)} %copy-done.3, ...), custom_call_target="tpu_custom_call" | custom-call | tf_op jit(solution)/shard_map/pallas_call | solution.py:447
  22.1 17.4 %all_to_all.5.got_ref = f32[16,8,128]{2,1,0:T(8,128)S(1)} all-to-all(f32[16,8,128]{2,1,0:T(8,128)S(1)} %get-tuple-element.24), channel_id=1, replica_groups=mesh['gx'=48,'gy'=16] {'gy'}, dimensions={0} | all-to-all | bytes 131072 | tf_op jit(solution)/shard_map/all_to_all | solution.py:456
  39.5 0.9 %shard_map.98 = (f32[3,32,16,128]{3,2,1,0:T(8,128)}, f32[3,32,16,128]{3,2,1,0:T(8,128)}, f32[1,2,32,256]{3,2,1,0:T(8,128)}) custom-call(f32[16,8,128]{2,1,0:T(8,128)S(1)} %all_to_all.5.got_ref, f32[3,4,16,128]{3,2,1,0:T(8,128)S(1)} %get-tuple-element.25.ee_ref, ...), custom_call_target="tpu_custom_call", output_to_operand_aliasing={{0}: (3, {}), {1}: (4, {})} | custom-call | tf_op jit(solution)/shard_map/pallas_call | solution.py:457
  (1 shorter events, 0.0 us)
Async XLA Ops:
  0.6 8.8 %copy-start = (f32[3,32,16,128]{3,2,1,0:T(8,128)S(1)}, f32[3,32,16,128]{3,2,1,0:T(8,128)}, u32[]{:S(2)}) copy-start(f32[3,32,16,128]{3,2,1,0:T(8,128)} %e_ref.5) | copy-start | bytes 2359300
  0.6 8.8 %copy-start.1 = (f32[3,32,16,128]{3,2,1,0:T(8,128)S(1)}, f32[3,32,16,128]{3,2,1,0:T(8,128)}, u32[]{:S(2)}) copy-start(f32[3,32,16,128]{3,2,1,0:T(8,128)} %h_ref.5) | copy-start | bytes 2359300
  2.0 7.5 %collective-permute-start = (f32[14,32,128]{2,1,0:T(8,128)S(1)}, f32[14,32,128]{2,1,0:T(8,128)S(1)}, u32[]{:S(2)}, u32[]{:S(2)}) collective-permute-start(f32[14,32,128]{2,1,0:T(8,128)S(1)} %get-tuple-element.17), channel_id=1, source_target_pairs={{1,2},{3,4},{5,6},{7,8},{9,10},{11,12},{13,14},{2,1},{4,3},{6,5},{... | collective-permute-start | bytes 688136 | tf_op jit(solution)/shard_map/ppermute | solution.py:32
  5.7 3.7 %copy-start.2 = (s32[32,16,128]{2,1,0:T(8,128)S(1)}, s32[32,16,128]{2,1,0:T(8,128)}, u32[]{:S(2)}) copy-start(s32[32,16,128]{2,1,0:T(8,128)} %m_ref.5) | copy-start | bytes 786436
  5.7 3.7 %copy-start.3 = (s32[32,16,128]{2,1,0:T(8,128)S(1)}, s32[32,16,128]{2,1,0:T(8,128)}, u32[]{:S(2)}) copy-start(s32[32,16,128]{2,1,0:T(8,128)} %p_ref.5) | copy-start | bytes 786436
  9.7 10.0 %collective-permute-start.1 = (f32[7,24,128]{2,1,0:T(8,128)S(1)}, f32[7,24,128]{2,1,0:T(8,128)S(1)}, u32[]{:S(2)}, u32[]{:S(2)}) collective-permute-start(f32[7,24,128]{2,1,0:T(8,128)S(1)} %get-tuple-element.20), channel_id=1, source_target_pairs={{16,32},{48,64},{80,96},{112,128},{144,160},{176,192},{208,224},{2... | collective-permute-start | bytes 258056 | tf_op jit(solution)/shard_map/ppermute | solution.py:32
  15.3 5.8 %collective-permute-start.2 = (f32[7,24,128]{2,1,0:T(8,128)S(1)}, f32[7,24,128]{2,1,0:T(8,128)S(1)}, u32[]{:S(2)}, u32[]{:S(2)}) collective-permute-start(f32[7,24,128]{2,1,0:T(8,128)S(1)} %get-tuple-element.21), channel_id=1, source_target_pairs={{0,16},{32,48},{64,80},{96,112},{128,144},{160,176},{192,208},{224... | collective-permute-start | bytes 258056 | tf_op jit(solution)/shard_map/ppermute | solution.py:32

commit v6 on v5

--- a/solution.py
+++ b/solution.py
@@ -216,8 +216,15 @@
         ez = keep * e[2][:rows] + gain * ((hy - h_last[1][:rows]) - (hx - hx_y))
         return ex, ey, ez
 
-    def run(self, planes, first, last, keep_first_step, store, skew, behind=None, ahead=None):
-        e0, h0, hc, ec, h1, e1, h2 = {}, {}, {}, {}, {}, {}, {}
+    def run(self, planes, first, last, keep_first_step, store, skew, behind=None, ahead=None, known=None, save=None):
+        e0, h0, hc, ec = {}, {}, {}, {}
+        h1, e1, h2 = known or ({}, {}, {})
+
+        def note(stage, x, value):
+            if save is not None:
+                save(stage, x, value)
+            return value
+
         begin = first - 2 if behind is None else first - 1
 
         def fetch(x):
@@ -240,11 +247,13 @@
             if begin <= x <= last - (ahead is not None):
                 fetch(x)
                 fetch(x + 1)
-                if e0[x] is None:
+                if x in h1:
+                    pass
+                elif e0[x] is None:
                     gain = hc[x][1]
                     h1[x] = (None, behind[Q_Y] + gain * e0[x + 1][2], behind[Q_Z] - gain * e0[x + 1][1])
                 else:
-                    h1[x] = self.h_step(h0[x], e0[x], e0[x + 1], hc[x], x > begin or behind is not None)
+                    h1[x] = note(0, x, self.h_step(h0[x], e0[x], e0[x + 1], hc[x], True))
             x = turn - skew
             if behind is not None and x == first - 1:
                 _, hy, hz = h1[x]
@@ -255,12 +264,13 @@
                 _, hy, hz = h1[x - 1]
                 e1[x] = (None, ahead[P_Y] + ahead[L_GAIN] * hz, ahead[P_Z] - ahead[L_GAIN] * hy)
             elif first - 1 <= x <= last:
-                e1[x] = self.e_step(e0[x], h1[x], h1[x - 1], ec[x])
+                if x not in e1:
+                    e1[x] = note(1, x, self.e_step(e0[x], h1[x], h1[x - 1], ec[x]))
                 if first <= x < last:
                     keep_first_step(x, e1[x])
             x = turn - 2 * skew - 1
-            if first - 1 <= x < last:
-                h2[x] = self.h_step(h1[x], e1[x], e1[x + 1], hc[x], x >= first)
+            if first - 1 <= x < last and x not in h2:
+                h2[x] = note(2, x, self.h_step(h1[x], e1[x], e1[x + 1], hc[x], h1[x][0] is not None))
             x = turn - 3 * skew - 1
             if first <= x < last:
                 store(x, self.e_step(e1[x], h2[x], h2[x - 1], ec[x], 16), h2[x])
@@ -286,7 +296,11 @@
     return out
 
 
-def inner_kernel(e_ref, h_ref, m_ref, p_ref, third_ref, table_ref, eo_hbm, ho_hbm, tile_ref, first_ref, eo_ref, ho_ref, sems):
+def saved_planes(nx):
+    return [(0, 0), (1, 1), (2, 1), (0, nx - 2), (1, nx - 2), (2, nx - 3)]
+
+
+def inner_kernel(e_ref, h_ref, m_ref, p_ref, third_ref, table_ref, eo_hbm, ho_hbm, tile_ref, saved_ref, first_ref, eo_ref, ho_ref, sems):
     refs = (e_ref, h_ref, m_ref, p_ref)
     nx = e_ref.shape[1]
 
@@ -310,7 +324,12 @@
                 copies.append(pltpu.make_async_copy(ref.at[:, part], hbm.at[:, part], sems.at[len(copies)]))
                 copies[-1].start()
 
-    for _ in Window(table_ref).run(planes, 2, nx - 2, keep_first_step, store, SKEW):
+    def save(stage, x, value):
+        if (stage, x) in saved_planes(nx):
+            for c in range(3):
+                saved_ref[saved_planes(nx).index((stage, x)), c] = value[c]
+
+    for _ in Window(table_ref).run(planes, 2, nx - 2, keep_first_step, store, SKEW, save=save):
         pass
     for step, ref in enumerate((first_ref, eo_ref)):
         tile_ref[step] = plane_tile(lambda c, x, half: ref[c, x, half * 8:half * 8 + 8, :], range(2, nx - 2))
@@ -318,7 +337,7 @@
         copy.wait()
 
 
-def edge_kernel(e_ref, h_ref, m_ref, p_ref, third_ref, outer_got, inner_got, table_ref, tile_ref, coef_ref,
+def edge_kernel(e_ref, h_ref, m_ref, p_ref, third_ref, outer_got, inner_got, table_ref, tile_ref, saved_ref, coef_ref,
                 eo_ref, ho_ref, part_ref, first_ref, right_ref, left_ref):
     refs = (e_ref, h_ref, m_ref, p_ref)
     nx = e_ref.shape[1]
@@ -350,8 +369,13 @@
             ho_ref[c, slot(x)] = h[c][0:16]
 
     window = Window(table_ref)
-    low = window.run(planes, 0, 2, keep_first_step, store, EDGE_SKEW, behind=right_ref)
-    high = window.run(planes, nx - 2, nx, keep_first_step, store, EDGE_SKEW, ahead=left_ref)
+    held = [tuple(saved_ref[k, c] for c in range(3)) for k in range(6)]
+    low_known = ({0: held[0], 1: None, 2: None}, {1: held[1], 2: None}, {1: held[2]})
+    high_known = (
+        {nx - 4: None, nx - 3: None, nx - 2: held[3]}, {nx - 3: None, nx - 2: held[4]}, {nx - 3: held[5]},
+    )
+    low = window.run(planes, 0, 2, keep_first_step, store, EDGE_SKEW, behind=right_ref, known=low_known)
+    high = window.run(planes, nx - 2, nx, keep_first_step, store, EDGE_SKEW, ahead=left_ref, known=high_known)
     for _ in zip(low, high):
         pass
     tiles = []
@@ -359,7 +383,8 @@
         edge = plane_tile(lambda c, x, half: ref[c, slot(x), half * 8:half * 8 + 8, :], (0, 1, nx - 2, nx - 1))
         tiles.append(tile_ref[step] + edge)
     for s in range(2 * NFREQ):
-        part_ref[s] = coef_ref[0, s] * tiles[0] + coef_ref[1, s] * tiles[1]
+        first_coef, second_coef = (jnp.broadcast_to(coef_ref[k:k + 1, s:s + 1], (8, 128)) for k in range(2))
+        part_ref[s] = first_coef * tiles[0] + second_coef * tiles[1]
 
 
 def last_kernel(got_ref, ee_ref, he_ref, _e, _h, eo_hbm, ho_hbm, spectra_hbm, out_ref, sems):
@@ -403,7 +428,6 @@
 EDGE_SKEW = 1
 CUTS = (10, 18, 26, 30)
 VM = pl.BlockSpec(memory_space=pltpu.VMEM)
-SM = pl.BlockSpec(memory_space=pltpu.SMEM)
 HBM = pl.BlockSpec(memory_space=pltpu.HBM)
 LIMIT = pltpu.CompilerParams(vmem_limit_bytes=16 << 20)
 
@@ -435,10 +459,10 @@
         in_specs=[VM] * 7, out_specs=(VM,) * 3, compiler_params=LIMIT,
     )(*fields, inner, outer, table)
     outer, inner = swapped(outer, "gx", 1), swapped(inner, "gx", 0)
-    ei, hi, tile = pl.pallas_call(
+    ei, hi, tile, saved = pl.pallas_call(
         inner_kernel,
-        out_shape=(whole, whole, shape(2, 8, 128)),
-        in_specs=[VM] * 6, out_specs=(HBM, HBM, VM),
+        out_shape=(whole, whole, shape(2, 8, 128), shape(6, 3, 24, nz)),
+        in_specs=[VM] * 6, out_specs=(HBM, HBM, VM, VM),
         scratch_shapes=[
             pltpu.VMEM((2, nx, ny, nz), jnp.float32), pltpu.VMEM((3, nx, ny, nz), jnp.float32),
             pltpu.VMEM((3, nx, ny, nz), jnp.float32), pltpu.SemaphoreType.DMA((2 * len(CUTS),)),
@@ -447,12 +471,12 @@
     ee, he, part = pl.pallas_call(
         edge_kernel,
         out_shape=(edge, edge, shape(2 * NFREQ, 8, 128)),
-        in_specs=[VM] * 9 + [SM], out_specs=(VM,) * 3,
+        in_specs=[VM] * 11, out_specs=(VM,) * 3,
         scratch_shapes=[
             pltpu.VMEM((2, 4, ny, nz), jnp.float32),
             pltpu.VMEM((X_MSG, 24, nz), jnp.float32), pltpu.VMEM((X_MSG, 24, nz), jnp.float32),
         ], compiler_params=LIMIT,
-    )(*fields, third, outer, inner, table, tile, coef)
+    )(*fields, third, outer, inner, table, tile, saved, coef)
     got = lax.all_to_all(part, "gy", split_axis=0, concat_axis=0, tiled=True)
     electric_out, magnetic_out, spectra = pl.pallas_call(
         last_kernel,

time: 40.6 us -> 40.1 us (0.988)
  Pallas kernels: 5.92 us -> 5.33 us
    pallas_call x1, Pallas kernels: 1.02 us -> 0.42 us  [local(): pl.pallas_call(edge_kernel, out_shape=(edge, edge, shape(2 * NFREQ, 8, 12...]
where the time goes in v6:
time: 40.1 us; the launch traced here: 39.8 us
  blocking collectives  19.6 us (49%)
  starting transfers between devices  11.3 us (28%)
  Pallas kernels  5.33 us (13%)
  waiting for transfers between devices  2.61 us (7%)
  between operations  0.74 us (2%)
    all_to_all x1, blocking collectives, local(): got = lax.all_to_all(part, 'gy', split_axis=0, concat_axis=0, tiled=True)  17.4 us
    ppermute x3, starting transfers between devices, swapped(): return lax.ppermute(x, axis, pairs + [(b, a) for a, b in pairs])  11.3 us
    ppermute x3, waiting for transfers between devices, swapped(): return lax.ppermute(x, axis, pairs + [(b, a) for a, b in pairs])  2.61 us
    pallas_call x1, Pallas kernels, local(): pl.pallas_call(inner_kernel, out_shape=(whole, whole, shape(2, 8, 128), s...  2.43 us
    all_gather x1, blocking collectives, gather_inner(): lax.all_gather(x, axis, axis=0, axis_index_groups=[list(p) for p in paire...  2.27 us
    pallas_call x1, Pallas kernels, local(): pl.pallas_call(rows_kernel, out_shape=(shape(MSG, nx, nz), shape(MSG, nx,...  1.3 us
    pallas_call x1, Pallas kernels, local(): pl.pallas_call(last_kernel, out_shape=(whole, whole, shape(1, 2, nx, 16 *...  0.9 us
  transfers between devices with their start and end apart: 3, of which 2 were waited for; matrix products, arithmetic and copies ran while one was open for 0% of the time, Pallas kernels for 6%

profile of v6, /device:TPU:513, one launch (start us, length us, event | category | flops | bytes accessed | tf_op | source)
XLA Modules:
  0.0 39.8 jit_solution(7060048761679270031)
XLA Ops:
  0.6 0.0 copy-start
  0.6 0.0 copy-start.1
  0.7 1.3 %shard_map.94 = (f32[14,32,128]{2,1,0:T(8,128)S(1)}, f32[14,32,128]{2,1,0:T(8,128)S(1)}, f32[16,128]{1,0:T(8,128)S(1)}, f32[1,8]{1,0:T(1,128)S(1)}) custom-call(f32[3,32,16,128]{3,2,1,0:T(8,128)} %e_ref.5, f32[3,32,16,128]{3,2,1,0:T(8,128)} %h_ref.5, s32[32,16,128]{2,1,0:T(8,128)} %m_ref.5, s32[32,16,128]{2,1,0:T(8,128)} %p_ref.5, f32[4]{0:T(128)} %eps_hbm.1, ...), custom_call_target="tpu_custom_call" | custom-call | tf_op jit(solution)/shard_map/pallas_call | solution.py:445
  2.0 3.8 %collective-permute-start = (f32[14,32,128]{2,1,0:T(8,128)S(1)}, f32[14,32,128]{2,1,0:T(8,128)S(1)}, u32[]{:S(2)}, u32[]{:S(2)}) collective-permute-start(f32[14,32,128]{2,1,0:T(8,128)S(1)} %get-tuple-element.18), channel_id=1, source_target_pairs={{1,2},{3,4},{5,6},{7,8},{9,10},{11,12},{13,14},{2,1},{4,3},{6,5},{... | collective-permute-start | bytes 688136 | tf_op jit(solution)/shard_map/ppermute | solution.py:32
  5.7 0.0 copy-start.2
  5.7 0.0 copy-start.3
  5.8 2.3 %all-gather = f32[28,32,128]{2,1,0:T(8,128)S(1)} all-gather(f32[14,32,128]{2,1,0:T(8,128)S(1)} %get-tuple-element.17), channel_id=2, replica_groups={{0,1},{2,3},{4,5},{6,7},{8,9},{10,11},{12,13},{14,15},{16,17},{18,19},{..., dimensions={0}, use_global_device_ids=true | all-gather | bytes 688128 | tf_op jit(solution)/shard_map/all_gather | solution.py:36
  8.0 0.1 multiply_cosine_fusion
  8.1 1.3 %collective-permute-done.outer_got = f32[14,32,128]{2,1,0:T(8,128)S(1)} collective-permute-done((f32[14,32,128]{2,1,0:T(8,128)S(1)}, f32[14,32,128]{2,1,0:T(8,128)S(1)}, u32[]{:S(2)}, u32[]{:S(2)}) %collective-permute-start) | collective-permute-done | bytes 229408 | tf_op jit(solution)/shard_map/ppermute | solution.py:32
  9.4 0.0 copy-done
  9.4 0.0 copy-done.1
  9.4 0.0 copy-done.2
  9.4 0.0 copy-done.3
  9.4 0.3 shard_map.95
  9.7 5.6 %collective-permute-start.1 = (f32[7,24,128]{2,1,0:T(8,128)S(1)}, f32[7,24,128]{2,1,0:T(8,128)S(1)}, u32[]{:S(2)}, u32[]{:S(2)}) collective-permute-start(f32[7,24,128]{2,1,0:T(8,128)S(1)} %get-tuple-element.21), channel_id=1, source_target_pairs={{16,32},{48,64},{80,96},{112,128},{144,160},{176,192},{208,224},{2... | collective-permute-start | bytes 258056 | tf_op jit(solution)/shard_map/ppermute | solution.py:32
  15.3 1.9 %collective-permute-start.2 = (f32[7,24,128]{2,1,0:T(8,128)S(1)}, f32[7,24,128]{2,1,0:T(8,128)S(1)}, u32[]{:S(2)}, u32[]{:S(2)}) collective-permute-start(f32[7,24,128]{2,1,0:T(8,128)S(1)} %get-tuple-element.22), channel_id=1, source_target_pairs={{0,16},{32,48},{64,80},{96,112},{128,144},{160,176},{192,208},{224... | collective-permute-start | bytes 258056 | tf_op jit(solution)/shard_map/ppermute | solution.py:32
  17.3 0.1 pad_maximum_fusion.coef_ref
  17.3 2.4 %shard_map.96 = (f32[3,32,16,128]{3,2,1,0:T(8,128)}, f32[3,32,16,128]{3,2,1,0:T(8,128)}, f32[2,8,128]{2,1,0:T(8,128)S(1)}, f32[6,3,24,128]{3,2,1,0:T(8,128)S(1)}) custom-call(f32[3,32,16,128]{3,2,1,0:T(8,128)S(1)} %copy-done, f32[3,32,16,128]{3,2,1,0:T(8,128)S(1)} %copy-done.1, s32[32,16,128]{2,1,0:T(8,128)S(1)} %copy-done.2, s32[32,16,128]{2,1,0:T(8,128)S(1)} %copy-done.3, ...), custom_call_target="tpu_custom_call" | custom-call | flops 41943040 | bytes 4194304 | tf_op jit(solution)/shard_map/pallas_call | solution.py:462
  19.8 0.0 collective-permute-done.1.outer_got
  19.8 1.3 %collective-permute-done.2.inner_got = f32[7,24,128]{2,1,0:T(8,128)S(1)} collective-permute-done((f32[7,24,128]{2,1,0:T(8,128)S(1)}, f32[7,24,128]{2,1,0:T(8,128)S(1)}, u32[]{:S(2)}, u32[]{:S(2)}) %collective-permute-start.2) | collective-permute-done | bytes 86048 | tf_op jit(solution)/shard_map/ppermute | solution.py:32
  21.1 0.4 %shard_map.97 = (f32[3,4,16,128]{3,2,1,0:T(8,128)S(1)}, f32[3,4,16,128]{3,2,1,0:T(8,128)S(1)}, f32[16,8,128]{2,1,0:T(8,128)S(1)}) custom-call(f32[3,32,16,128]{3,2,1,0:T(8,128)S(1)} %copy-done, f32[3,32,16,128]{3,2,1,0:T(8,128)S(1)} %copy-done.1, s32[32,16,128]{2,1,0:T(8,128)S(1)} %copy-done.2, s32[32,16,128]{2,1,0:T(8,128)S(1)} %copy-done.3, ...), custom_call_target="tpu_custom_call" | custom-call | tf_op jit(solution)/shard_map/pallas_call | solution.py:471
  21.5 17.4 %all_to_all.5.got_ref = f32[16,8,128]{2,1,0:T(8,128)S(1)} all-to-all(f32[16,8,128]{2,1,0:T(8,128)S(1)} %get-tuple-element.26), channel_id=1, replica_groups=mesh['gx'=48,'gy'=16] {'gy'}, dimensions={0} | all-to-all | bytes 131072 | tf_op jit(solution)/shard_map/all_to_all | solution.py:480
  38.9 0.9 %shard_map.98 = (f32[3,32,16,128]{3,2,1,0:T(8,128)}, f32[3,32,16,128]{3,2,1,0:T(8,128)}, f32[1,2,32,256]{3,2,1,0:T(8,128)}) custom-call(f32[16,8,128]{2,1,0:T(8,128)S(1)} %all_to_all.5.got_ref, f32[3,4,16,128]{3,2,1,0:T(8,128)S(1)} %get-tuple-element.27.ee_ref, ...), custom_call_target="tpu_custom_call", output_to_operand_aliasing={{0}: (3, {}), {1}: (4, {})} | custom-call | tf_op jit(solution)/shard_map/pallas_call | solution.py:481
  (1 shorter events, 0.0 us)
Async XLA Ops:
  0.6 8.8 %copy-start = (f32[3,32,16,128]{3,2,1,0:T(8,128)S(1)}, f32[3,32,16,128]{3,2,1,0:T(8,128)}, u32[]{:S(2)}) copy-start(f32[3,32,16,128]{3,2,1,0:T(8,128)} %e_ref.5) | copy-start | bytes 2359300
  0.6 8.8 %copy-start.1 = (f32[3,32,16,128]{3,2,1,0:T(8,128)S(1)}, f32[3,32,16,128]{3,2,1,0:T(8,128)}, u32[]{:S(2)}) copy-start(f32[3,32,16,128]{3,2,1,0:T(8,128)} %h_ref.5) | copy-start | bytes 2359300
  2.0 7.5 %collective-permute-start = (f32[14,32,128]{2,1,0:T(8,128)S(1)}, f32[14,32,128]{2,1,0:T(8,128)S(1)}, u32[]{:S(2)}, u32[]{:S(2)}) collective-permute-start(f32[14,32,128]{2,1,0:T(8,128)S(1)} %get-tuple-element.18), channel_id=1, source_target_pairs={{1,2},{3,4},{5,6},{7,8},{9,10},{11,12},{13,14},{2,1},{4,3},{6,5},{... | collective-permute-start | bytes 688136 | tf_op jit(solution)/shard_map/ppermute | solution.py:32
  5.7 3.7 %copy-start.2 = (s32[32,16,128]{2,1,0:T(8,128)S(1)}, s32[32,16,128]{2,1,0:T(8,128)}, u32[]{:S(2)}) copy-start(s32[32,16,128]{2,1,0:T(8,128)} %m_ref.5) | copy-start | bytes 786436
  5.7 3.7 %copy-start.3 = (s32[32,16,128]{2,1,0:T(8,128)S(1)}, s32[32,16,128]{2,1,0:T(8,128)}, u32[]{:S(2)}) copy-start(s32[32,16,128]{2,1,0:T(8,128)} %p_ref.5) | copy-start | bytes 786436
  9.7 10.0 %collective-permute-start.1 = (f32[7,24,128]{2,1,0:T(8,128)S(1)}, f32[7,24,128]{2,1,0:T(8,128)S(1)}, u32[]{:S(2)}, u32[]{:S(2)}) collective-permute-start(f32[7,24,128]{2,1,0:T(8,128)S(1)} %get-tuple-element.21), channel_id=1, source_target_pairs={{16,32},{48,64},{80,96},{112,128},{144,160},{176,192},{208,224},{2... | collective-permute-start | bytes 258056 | tf_op jit(solution)/shard_map/ppermute | solution.py:32
  15.3 5.8 %collective-permute-start.2 = (f32[7,24,128]{2,1,0:T(8,128)S(1)}, f32[7,24,128]{2,1,0:T(8,128)S(1)}, u32[]{:S(2)}, u32[]{:S(2)}) collective-permute-start(f32[7,24,128]{2,1,0:T(8,128)S(1)} %get-tuple-element.22), channel_id=1, source_target_pairs={{0,16},{32,48},{64,80},{96,112},{128,144},{160,176},{192,208},{224... | collective-permute-start | bytes 258056 | tf_op jit(solution)/shard_map/ppermute | solution.py:32

commit v7 on v6

--- a/solution.py
+++ b/solution.py
@@ -54,8 +54,20 @@
                 inner_ref, outer_ref, table_ref, omega_ref, up_codes, down_codes, sigma_ref, eps_ref, sems):
     ny = m_hbm.shape[1]
 
+    def make_tables():
+        sigma = sigma_ref[...]
+        s_mag = sigma * time_step / 2.0
+        table_ref[0:1] = (1.0 - s_mag) / (1.0 + s_mag)
+        table_ref[1:2] = time_step / (1.0 + s_mag)
+        for k in range(NMAT):
+            eps = jnp.full((1, 128), eps_ref[k], jnp.float32)
+            s_ele = sigma * time_step / (2.0 * eps)
+            table_ref[2 + k:3 + k] = (1.0 - s_ele) / (1.0 + s_ele)
+            table_ref[6 + k:7 + k] = time_step / (eps * (1.0 + s_ele))
+            table_ref[10 + k:11 + k] = time_step / eps
+
     def fetch(up_ref, down_ref):
-        pairs = []
+        pairs = [(eps_hbm, eps_ref), (sigma_hbm, sigma_ref)]
         for ref, last in ((up_ref, ny - 1), (down_ref, 0)):
             pairs += [(e_hbm.at[:, :, last, :], ref.at[0:3]), (h_hbm.at[:, :, last, :], ref.at[3:6])]
         pairs += [
@@ -65,12 +77,15 @@
             (e_hbm.at[:, :, ny - 2, :], up_ref.at[8:11]),
             (h_hbm.at[0, :, ny - 2, :], up_ref.at[11]), (h_hbm.at[2, :, ny - 2, :], up_ref.at[12]),
             (e_hbm.at[0, :, 1, :], down_ref.at[8]), (e_hbm.at[2, :, 1, :], down_ref.at[9]),
-            (eps_hbm, eps_ref), (sigma_hbm, sigma_ref), (omega_hbm, omega_ref),
+            (omega_hbm, omega_ref),
         ]
         copies = [pltpu.make_async_copy(src, dst, sems.at[i]) for i, (src, dst) in enumerate(pairs)]
         for copy in copies:
             copy.start()
-        for copy in copies:
+        for copy in copies[:2]:
+            copy.wait()
+        make_tables()
+        for copy in copies[2:]:
             copy.wait()
         up_ref[6:8] = up_codes[0:2].astype(jnp.float32) + 1.0
         up_ref[13] = up_codes[2].astype(jnp.float32) + 1.0
@@ -85,17 +100,6 @@
     @pl.when(second == 1)
     def _():
         fetch(outer_ref, inner_ref)
-
-    sigma = sigma_ref[...]
-    s_mag = sigma * time_step / 2.0
-    table_ref[0:1] = (1.0 - s_mag) / (1.0 + s_mag)
-    table_ref[1:2] = time_step / (1.0 + s_mag)
-    for k in range(NMAT):
-        eps = jnp.full((1, 128), eps_ref[k], jnp.float32)
-        s_ele = sigma * time_step / (2.0 * eps)
-        table_ref[2 + k:3 + k] = (1.0 - s_ele) / (1.0 + s_ele)
-        table_ref[6 + k:7 + k] = time_step / (eps * (1.0 + s_ele))
-        table_ref[10 + k:11 + k] = time_step / eps
 
 
 def planes_kernel(e_ref, h_ref, m_ref, p_ref, inner_got, outer_got, table_ref, inner_ref, outer_ref, third_ref):

time: 40.1 us -> 40 us (level)
  no operation moved by 1% of the time
where the time goes in v7:
time: 40 us; the launch traced here: 39.8 us
  blocking collectives  19.6 us (49%)
  starting transfers between devices  11.3 us (28%)
  Pallas kernels  5.31 us (13%)
  waiting for transfers between devices  2.61 us (7%)
  between operations  0.74 us (2%)
    all_to_all x1, blocking collectives, local(): got = lax.all_to_all(part, 'gy', split_axis=0, concat_axis=0, tiled=True)  17.4 us
    ppermute x3, starting transfers between devices, swapped(): return lax.ppermute(x, axis, pairs + [(b, a) for a, b in pairs])  11.3 us
    ppermute x3, waiting for transfers between devices, swapped(): return lax.ppermute(x, axis, pairs + [(b, a) for a, b in pairs])  2.61 us
    pallas_call x1, Pallas kernels, local(): pl.pallas_call(inner_kernel, out_shape=(whole, whole, shape(2, 8, 128), s...  2.43 us
    all_gather x1, blocking collectives, gather_inner(): lax.all_gather(x, axis, axis=0, axis_index_groups=[list(p) for p in paire...  2.27 us
    pallas_call x1, Pallas kernels, local(): pl.pallas_call(rows_kernel, out_shape=(shape(MSG, nx, nz), shape(MSG, nx,...  1.28 us
    pallas_call x1, Pallas kernels, local(): pl.pallas_call(last_kernel, out_shape=(whole, whole, shape(1, 2, nx, 16 *...  0.9 us
  transfers between devices with their start and end apart: 3, of which 2 were waited for; matrix products, arithmetic and copies ran while one was open for 0% of the time, Pallas kernels for 6%

profile of v7, /device:TPU:513, one launch (start us, length us, event | category | flops | bytes accessed | tf_op | source)
XLA Modules:
  0.0 39.8 jit_solution(7194900273342230617)
XLA Ops:
  0.6 0.0 copy-start
  0.6 0.0 copy-start.1
  0.7 1.3 %shard_map.94 = (f32[14,32,128]{2,1,0:T(8,128)S(1)}, f32[14,32,128]{2,1,0:T(8,128)S(1)}, f32[16,128]{1,0:T(8,128)S(1)}, f32[1,8]{1,0:T(1,128)S(1)}) custom-call(f32[3,32,16,128]{3,2,1,0:T(8,128)} %e_ref.5, f32[3,32,16,128]{3,2,1,0:T(8,128)} %h_ref.5, s32[32,16,128]{2,1,0:T(8,128)} %m_ref.5, s32[32,16,128]{2,1,0:T(8,128)} %p_ref.5, f32[4]{0:T(128)} %eps_hbm.1, ...), custom_call_target="tpu_custom_call" | custom-call | tf_op jit(solution)/shard_map/pallas_call | solution.py:449
  1.9 3.8 %collective-permute-start = (f32[14,32,128]{2,1,0:T(8,128)S(1)}, f32[14,32,128]{2,1,0:T(8,128)S(1)}, u32[]{:S(2)}, u32[]{:S(2)}) collective-permute-start(f32[14,32,128]{2,1,0:T(8,128)S(1)} %get-tuple-element.18), channel_id=1, source_target_pairs={{1,2},{3,4},{5,6},{7,8},{9,10},{11,12},{13,14},{2,1},{4,3},{6,5},{... | collective-permute-start | bytes 688136 | tf_op jit(solution)/shard_map/ppermute | solution.py:32
  5.7 0.0 copy-start.2
  5.7 0.0 copy-start.3
  5.7 2.3 %all-gather = f32[28,32,128]{2,1,0:T(8,128)S(1)} all-gather(f32[14,32,128]{2,1,0:T(8,128)S(1)} %get-tuple-element.17), channel_id=2, replica_groups={{0,1},{2,3},{4,5},{6,7},{8,9},{10,11},{12,13},{14,15},{16,17},{18,19},{..., dimensions={0}, use_global_device_ids=true | all-gather | bytes 688128 | tf_op jit(solution)/shard_map/all_gather | solution.py:36
  8.0 0.1 multiply_cosine_fusion
  8.1 1.3 %collective-permute-done.outer_got = f32[14,32,128]{2,1,0:T(8,128)S(1)} collective-permute-done((f32[14,32,128]{2,1,0:T(8,128)S(1)}, f32[14,32,128]{2,1,0:T(8,128)S(1)}, u32[]{:S(2)}, u32[]{:S(2)}) %collective-permute-start) | collective-permute-done | bytes 229408 | tf_op jit(solution)/shard_map/ppermute | solution.py:32
  9.4 0.0 copy-done
  9.4 0.0 copy-done.1
  9.4 0.0 copy-done.2
  9.4 0.0 copy-done.3
  9.4 0.3 shard_map.95
  9.7 5.6 %collective-permute-start.1 = (f32[7,24,128]{2,1,0:T(8,128)S(1)}, f32[7,24,128]{2,1,0:T(8,128)S(1)}, u32[]{:S(2)}, u32[]{:S(2)}) collective-permute-start(f32[7,24,128]{2,1,0:T(8,128)S(1)} %get-tuple-element.21), channel_id=1, source_target_pairs={{16,32},{48,64},{80,96},{112,128},{144,160},{176,192},{208,224},{2... | collective-permute-start | bytes 258056 | tf_op jit(solution)/shard_map/ppermute | solution.py:32
  15.3 1.9 %collective-permute-start.2 = (f32[7,24,128]{2,1,0:T(8,128)S(1)}, f32[7,24,128]{2,1,0:T(8,128)S(1)}, u32[]{:S(2)}, u32[]{:S(2)}) collective-permute-start(f32[7,24,128]{2,1,0:T(8,128)S(1)} %get-tuple-element.22), channel_id=1, source_target_pairs={{0,16},{32,48},{64,80},{96,112},{128,144},{160,176},{192,208},{224... | collective-permute-start | bytes 258056 | tf_op jit(solution)/shard_map/ppermute | solution.py:32
  17.2 0.1 pad_maximum_fusion.coef_ref
  17.3 2.4 %shard_map.96 = (f32[3,32,16,128]{3,2,1,0:T(8,128)}, f32[3,32,16,128]{3,2,1,0:T(8,128)}, f32[2,8,128]{2,1,0:T(8,128)S(1)}, f32[6,3,24,128]{3,2,1,0:T(8,128)S(1)}) custom-call(f32[3,32,16,128]{3,2,1,0:T(8,128)S(1)} %copy-done, f32[3,32,16,128]{3,2,1,0:T(8,128)S(1)} %copy-done.1, s32[32,16,128]{2,1,0:T(8,128)S(1)} %copy-done.2, s32[32,16,128]{2,1,0:T(8,128)S(1)} %copy-done.3, ...), custom_call_target="tpu_custom_call" | custom-call | flops 41943040 | bytes 4194304 | tf_op jit(solution)/shard_map/pallas_call | solution.py:466
  19.7 0.0 collective-permute-done.1.outer_got
  19.8 1.3 %collective-permute-done.2.inner_got = f32[7,24,128]{2,1,0:T(8,128)S(1)} collective-permute-done((f32[7,24,128]{2,1,0:T(8,128)S(1)}, f32[7,24,128]{2,1,0:T(8,128)S(1)}, u32[]{:S(2)}, u32[]{:S(2)}) %collective-permute-start.2) | collective-permute-done | bytes 86048 | tf_op jit(solution)/shard_map/ppermute | solution.py:32
  21.1 0.4 %shard_map.97 = (f32[3,4,16,128]{3,2,1,0:T(8,128)S(1)}, f32[3,4,16,128]{3,2,1,0:T(8,128)S(1)}, f32[16,8,128]{2,1,0:T(8,128)S(1)}) custom-call(f32[3,32,16,128]{3,2,1,0:T(8,128)S(1)} %copy-done, f32[3,32,16,128]{3,2,1,0:T(8,128)S(1)} %copy-done.1, s32[32,16,128]{2,1,0:T(8,128)S(1)} %copy-done.2, s32[32,16,128]{2,1,0:T(8,128)S(1)} %copy-done.3, ...), custom_call_target="tpu_custom_call" | custom-call | tf_op jit(solution)/shard_map/pallas_call | solution.py:475
  21.5 17.4 %all_to_all.5.got_ref = f32[16,8,128]{2,1,0:T(8,128)S(1)} all-to-all(f32[16,8,128]{2,1,0:T(8,128)S(1)} %get-tuple-element.26), channel_id=1, replica_groups=mesh['gx'=48,'gy'=16] {'gy'}, dimensions={0} | all-to-all | bytes 131072 | tf_op jit(solution)/shard_map/all_to_all | solution.py:484
  38.9 0.9 %shard_map.98 = (f32[3,32,16,128]{3,2,1,0:T(8,128)}, f32[3,32,16,128]{3,2,1,0:T(8,128)}, f32[1,2,32,256]{3,2,1,0:T(8,128)}) custom-call(f32[16,8,128]{2,1,0:T(8,128)S(1)} %all_to_all.5.got_ref, f32[3,4,16,128]{3,2,1,0:T(8,128)S(1)} %get-tuple-element.27.ee_ref, ...), custom_call_target="tpu_custom_call", output_to_operand_aliasing={{0}: (3, {}), {1}: (4, {})} | custom-call | tf_op jit(solution)/shard_map/pallas_call | solution.py:485
  (1 shorter events, 0.0 us)
Async XLA Ops:
  0.6 8.8 %copy-start = (f32[3,32,16,128]{3,2,1,0:T(8,128)S(1)}, f32[3,32,16,128]{3,2,1,0:T(8,128)}, u32[]{:S(2)}) copy-start(f32[3,32,16,128]{3,2,1,0:T(8,128)} %e_ref.5) | copy-start | bytes 2359300
  0.6 8.8 %copy-start.1 = (f32[3,32,16,128]{3,2,1,0:T(8,128)S(1)}, f32[3,32,16,128]{3,2,1,0:T(8,128)}, u32[]{:S(2)}) copy-start(f32[3,32,16,128]{3,2,1,0:T(8,128)} %h_ref.5) | copy-start | bytes 2359300
  1.9 7.5 %collective-permute-start = (f32[14,32,128]{2,1,0:T(8,128)S(1)}, f32[14,32,128]{2,1,0:T(8,128)S(1)}, u32[]{:S(2)}, u32[]{:S(2)}) collective-permute-start(f32[14,32,128]{2,1,0:T(8,128)S(1)} %get-tuple-element.18), channel_id=1, source_target_pairs={{1,2},{3,4},{5,6},{7,8},{9,10},{11,12},{13,14},{2,1},{4,3},{6,5},{... | collective-permute-start | bytes 688136 | tf_op jit(solution)/shard_map/ppermute | solution.py:32
  5.7 3.7 %copy-start.2 = (s32[32,16,128]{2,1,0:T(8,128)S(1)}, s32[32,16,128]{2,1,0:T(8,128)}, u32[]{:S(2)}) copy-start(s32[32,16,128]{2,1,0:T(8,128)} %m_ref.5) | copy-start | bytes 786436
  5.7 3.7 %copy-start.3 = (s32[32,16,128]{2,1,0:T(8,128)S(1)}, s32[32,16,128]{2,1,0:T(8,128)}, u32[]{:S(2)}) copy-start(s32[32,16,128]{2,1,0:T(8,128)} %p_ref.5) | copy-start | bytes 786436
  9.7 10.0 %collective-permute-start.1 = (f32[7,24,128]{2,1,0:T(8,128)S(1)}, f32[7,24,128]{2,1,0:T(8,128)S(1)}, u32[]{:S(2)}, u32[]{:S(2)}) collective-permute-start(f32[7,24,128]{2,1,0:T(8,128)S(1)} %get-tuple-element.21), channel_id=1, source_target_pairs={{16,32},{48,64},{80,96},{112,128},{144,160},{176,192},{208,224},{2... | collective-permute-start | bytes 258056 | tf_op jit(solution)/shard_map/ppermute | solution.py:32
  15.3 5.8 %collective-permute-start.2 = (f32[7,24,128]{2,1,0:T(8,128)S(1)}, f32[7,24,128]{2,1,0:T(8,128)S(1)}, u32[]{:S(2)}, u32[]{:S(2)}) collective-permute-start(f32[7,24,128]{2,1,0:T(8,128)S(1)} %get-tuple-element.22), channel_id=1, source_target_pairs={{0,16},{32,48},{64,80},{96,112},{128,144},{160,176},{192,208},{224... | collective-permute-start | bytes 258056 | tf_op jit(solution)/shard_map/ppermute | solution.py:32
